TPU v7x, 32 devices: a whole 2x2x4 slice. The times are simulated.
32 devices in a mesh: dp: 2 (over x), ha: 4 (over z), wa: 4 (over y, core).
Axes of the slice: x: 2, y: 2, z: 4, core: 2. Of those that a mesh axis runs over, the one named last changes fastest.
Arguments:
- query_in: bfloat16 [2, 4, 4, 384, 512], P('dp', 'ha', 'wa'), may hold values from -30 to 30
- key_in: bfloat16 [2, 4, 4, 384, 512], P('dp', 'ha', 'wa'), may hold values from -6 to 6
- value_in: bfloat16 [2, 4, 4, 384, 512], P('dp', 'ha', 'wa'), may hold values from -6 to 6
- grad_out: bfloat16 [2, 4, 4, 384, 3072], P('dp', 'ha', 'wa'), may hold values from -1.5 to 1.5
- out_weight: bfloat16 [512, 3072], P('dp'), may hold values from -0.25 to 0.25
Outputs:
- outcome: bfloat16 [2, 4, 4, 384, 3072], P('dp', 'ha', 'wa')
- query_grad: float32 [2, 4, 4, 384, 512], P('dp', 'ha', 'wa')
- key_grad: float32 [2, 4, 4, 384, 512], P('dp', 'ha', 'wa')
- value_grad: float32 [2, 4, 4, 384, 512], P('dp', 'ha', 'wa')
- weight_grad: float32 [512, 3072], P('dp')
All inputs are finite; a program needn't handle non-finite values.
Results may differ from a plain program's by a relative error of at most 0.035.
Values may be sent and summed in bfloat16 or wider, within the bound.
No kernel may reach another device: no remote copies, remote signals or barrier semaphores. Data moves between devices by JAX's collectives and lax.ppermute only.
A program may use at most 192 MiB of HBM per device.

v0:
```python
import math

import jax
import jax.numpy as jnp
from jax import lax
from jax.experimental import pallas as pl
from jax.experimental.pallas import tpu as pltpu
from jax.sharding import PartitionSpec as P


HEADS = 4
BF = jnp.bfloat16
F32 = jnp.float32


def xor_send(value, axis, mask):
    count = lax.axis_size(axis)
    return lax.ppermute(value, axis, [(i, i ^ mask) for i in range(count)])


def step_send(value, axis, step):
    count = lax.axis_size(axis)
    pairs = [(i, i + step) for i in range(count) if 0 <= i + step < count]
    return lax.ppermute(value, axis, pairs)


def sds(shape, dtype):
    return jax.ShapeDtypeStruct(shape, dtype)


def full_spec(shape):
    zeros = (0,) * len(shape)
    return pl.BlockSpec(tuple(shape), lambda *_: zeros)


def place_of():
    d, h, w = lax.axis_index("dp"), lax.axis_index("ha"), lax.axis_index("wa")
    core, yy = w & 1, w >> 1
    heads_at = (0, 1, 2, 3)
    if lax.axis_size("dp") == 2:
        heads_at = (2 * d, 2 * d + 1, 2 - 2 * d, 3 - 2 * d)
    row_lo = jnp.where(h > 0, 0, 1)
    row_hi = jnp.where(h < lax.axis_size("ha") - 1, 3, 2)
    return (w, *heads_at, row_lo, row_hi, d, yy, h, core)


def call(kernel, args, outs, grid=(1,), in_specs=None, out_specs=None, scratch=(), flops=0, exps=0, alias=None):
    in_specs = [full_spec(a.shape) if s is None else s for a, s in zip(args, in_specs or [None] * len(args))]
    out_specs = [full_spec(o.shape) if s is None else s for o, s in zip(outs, out_specs or [None] * len(outs))]
    moved = sum(a.size * a.dtype.itemsize for a in args) + sum(o.size * jnp.dtype(o.dtype).itemsize for o in outs)
    return pl.pallas_call(
        lambda *refs: kernel(place_of(), *refs),
        out_shape=list(outs),
        grid=grid,
        in_specs=in_specs,
        out_specs=out_specs,
        scratch_shapes=list(scratch),
        input_output_aliases=alias or {},
        cost_estimate=pl.CostEstimate(flops=flops, transcendentals=exps, bytes_accessed=moved),
        compiler_params=pltpu.CompilerParams(
            dimension_semantics=("arbitrary",) * len(grid), vmem_limit_bytes=56 << 20
        ),
    )(*args)


def dot(a, b, dims):
    return lax.dot_general(a, b, (dims, ((), ())), preferred_element_type=F32)


NN = ((1,), (0,))
NT = ((1,), (1,))
TN = ((0,), (0,))


def lanes(index, width=128):
    return pl.ds(pl.multiple_of(index * width, width), width)


def pack_kernel(sc, q, k, v, *outs):
    w = sc[0]
    for far in range(2):
        for j in range(2):
            cols = lanes(w ^ (2 * far + j))
            outs[far][j, 0] = k[:, cols]
            outs[far][j, 1] = v[:, cols]
            outs[2 + far][j] = q[:, cols]


def stack_rows(core, own, even, odd, whole):
    size = own.shape[0]
    whole[:size, :] = own[...]

    @pl.when(core == 0)
    def _():
        whole[size:, :] = even[...]

    @pl.when(core == 1)
    def _():
        whole[size:, :] = odd[...]

    return whole[...]


def grad_attn_kernel(sc, g, w_own, w_even, w_odd, near, far, acc, by_head, whole):
    step = pl.program_id(0)
    part = dot(g[...], stack_rows(sc[10], w_own, w_even, w_odd, whole), NT)

    @pl.when(step == 0)
    def _():
        acc[...] = part

    @pl.when(step > 0)
    def _():
        acc[...] += part

    @pl.when(step == pl.num_programs(0) - 1)
    def _():
        for slot in range(4):
            by_head[sc[1 + slot]] = acc[:, slot * 128 : slot * 128 + 128].astype(BF)
        for j in range(2):
            near[j] = by_head[sc[0] ^ j]
            far[j] = by_head[sc[0] ^ (2 + j)]


def tile_rows_at(index, tile):
    return pl.ds(pl.multiple_of(index * tile, tile), tile)


def forward_kernel(factor, sc, *refs):
    q_in, kv_in = refs[:4], refs[4:16]
    near, far, att_b, inv_b, p_b = refs[16:21]
    ks, vs, qs, ss, mx, acc = refs[21:]
    tile = mx.shape[0]
    w, row_lo, row_hi = sc[0], sc[5], sc[6]
    step = pl.program_id(0)

    @pl.when(step == 0)
    def _():
        for m in range(4):
            at = tile_rows_at(w ^ m, tile)
            qs[at, :] = q_in[m][0]
            for r in range(3):
                ks[r, at, :] = kv_in[r * 4 + m][0, 0]
                vs[r, at, :128] = kv_in[r * 4 + m][0, 1]
                vs[r, at, 128:] = jnp.ones((tile, 128), BF)

    def one_tile(b):
        start, stop = max(b - 1, 0) * tile, min(b + 2, 4) * tile
        width = stop - start
        q = qs[b * tile : b * tile + tile, :]
        mx[...] = jnp.full(mx.shape, -jnp.inf, F32)

        def score_row(r, carry):
            s = dot(q, ks[r, start:stop, :], NT)
            ss[r, :, :width] = s
            best = mx[...]
            for i in range(width // 128):
                best = jnp.maximum(best, s[:, i * 128 : i * 128 + 128])
            mx[...] = best
            return carry

        lax.fori_loop(row_lo, row_hi, score_row, 0)
        top = jnp.max(mx[...], axis=1, keepdims=True)
        acc[...] = jnp.zeros_like(acc)

        def prob_row(r, carry):
            p = jnp.exp2((ss[r, :, :width] - top) * factor).astype(BF)
            p_b[0, r, :, :width] = p
            acc[...] += dot(p, vs[r, start:stop, :], NN)
            return carry

        lax.fori_loop(row_lo, row_hi, prob_row, 0)

    for b in range(4):
        pl.when(step == b)(lambda b=b: one_tile(b))
    inverse = 1.0 / acc[:, 128:]
    out = (acc[:, :128] * inverse).astype(BF)
    att_b[0] = out
    inv_b[0] = inverse
    for m in range(4):

        @pl.when((step ^ w) == m)
        def _():
            (near, far)[m // 2][m % 2] = out


def backward_kernel(row, scale, sc, *refs):
    q_in, kv_in, do_in = refs[:4], refs[4:8], refs[8:12]
    att_b, inv_b, p_in = refs[12:15]
    rest = refs[15:]
    dq_prev = None
    if row != 0:
        dq_prev, rest = rest[0], rest[1:]
    if row == 1:
        dq_near, dq_far, dkv_out, rest = rest[0], rest[1], rest[2], rest[3:]
    else:
        dq_out, dkv_out, rest = rest[0], rest[1], rest[2:]
    ks, vs, qs, dos, dk, dv, dq = rest
    tile = dq.shape[0]
    step = pl.program_id(0)
    w, row_lo, row_hi = sc[0], sc[5], sc[6]

    @pl.when(step == 0)
    def _():
        for m in range(4):
            at = tile_rows_at(w ^ m, tile)
            qs[at, :] = q_in[m][0]
            dos[at, :] = do_in[m][0]
            ks[at, :] = kv_in[m][0, 0]
            vs[at, :] = kv_in[m][0, 1]
        dk[...] = jnp.zeros_like(dk)
        dv[...] = jnp.zeros_like(dv)

    dq[...] = jnp.zeros_like(dq) if dq_prev is None else dq_prev[0]
    inverse = inv_b[0]
    here = tile_rows_at(step, tile)
    grad = dos[here, :].astype(F32)
    delta = jnp.sum(att_b[0].astype(F32) * grad, axis=1, keepdims=True) * inverse[:, :1]
    grad = (grad * inverse).astype(BF)
    q = qs[here, :]

    def one_tile(b):
        start, stop = max(b - 1, 0) * tile, min(b + 2, 4) * tile
        p = p_in[0, 0, :, : stop - start]
        dp = dot(grad, vs[start:stop, :], NT)
        ds = (p.astype(F32) * (dp - delta)).astype(BF)
        dq[...] += dot(ds, ks[start:stop, :], NN)
        dk[:, start:stop] += dot(q, ds, TN)
        dv[:, start:stop] += dot(grad, p, TN)

    valid = (row_lo <= row) & (row < row_hi)
    for b in range(4):
        pl.when((step == b) & valid)(lambda b=b: one_tile(b))

    if row != 1:
        dq_out[0] = dq[...]
    else:
        total = (dq[...] * scale).astype(BF)
        for m in range(4):

            @pl.when((step ^ w) == m)
            def _():
                (dq_near, dq_far)[m // 2][m % 2] = total

    @pl.when(step == pl.num_programs(0) - 1)
    def _():
        dkv_out[0] = (dk[...] * scale).T.astype(dkv_out.dtype)
        dkv_out[1] = dv[...].T.astype(dkv_out.dtype)


def combine_kernel(sc, own, above, below, near, far):
    tile = near.shape[2]
    for m in range(4):
        at = tile_rows_at(sc[0] ^ m, tile)
        for i in range(2):
            total = own[i, at, :] + above[i, at, :].astype(F32) + below[i, at, :].astype(F32)
            (near, far)[m // 2][m % 2, i] = total.astype(BF)


def finish_kernel(sc, *refs):
    dq_in, dkv_in, (dq, dk, dv) = refs[:4], refs[4:8], refs[8:]
    for m in range(4):
        cols = lanes(sc[0] ^ m)
        dq[:, cols] = dq_in[m][0].astype(F32)
        dk[:, cols] = dkv_in[m][0, 0].astype(F32)
        dv[:, cols] = dkv_in[m][0, 1].astype(F32)


def outcome_kernel(sc, near, p_near, far, p_far, w_own, w_even, w_odd, out, att, slots, whole):
    @pl.when(pl.program_id(0) == 0)
    def _():
        for m, piece in enumerate((near, p_near, far, p_far)):
            att[sc[0] ^ m] = piece[0]
        for slot in range(4):
            slots[:, slot * 128 : slot * 128 + 128] = att[sc[1 + slot]]

    out[...] = dot(slots[...], stack_rows(sc[10], w_own, w_even, w_odd, whole), NN).astype(BF)


def weight_kernel(sc, near, far, p_near, p_far, g, g_other, a_own, a_send, b_keep, b_send, att, slots, both, res):
    tile = g.shape[0]
    step = pl.program_id(0)
    w, d, yy = sc[0], sc[7], sc[8]

    @pl.when(step == 0)
    def _():
        for t in range(2):
            at = slice(t * tile, t * tile + tile)
            att[w, at, :] = near[t]
            att[w ^ 2, at, :] = far[t]
            att[w ^ 1, at, :] = p_near[1 - t]
            att[w ^ 3, at, :] = p_far[1 - t]
        for slot in range(4):
            slots[slot * 128 : slot * 128 + 128, :] = att[2 * (d ^ (slot // 2)) + slot % 2].T

    both[:tile, :] = g[...]
    both[tile:, :] = g_other[...]
    total = dot(slots[...], both[...], NN)

    @pl.when(step == 0)
    def _():
        a_own[...] = total[:256, :]
        a_send[...] = total[256:, :].astype(BF)

    @pl.when(step == 1)
    def _():
        res[...] = total
        for i in range(2):
            at = slice(i * 128, i * 128 + 128)
            b_keep[at, :] = res[lanes(2 * i + yy), :]
            b_send[at, :] = res[lanes(2 * i + 1 - yy), :].astype(BF)


def reduce_first_kernel(sc, a_own, a_in, b_keep, b_in, a_keep, a_send, b_own, b_send):
    yy = sc[8]
    mine, theirs = lanes(yy), lanes(1 - yy)
    a_keep[...] = a_own[mine, :] + a_in[mine, :].astype(F32)
    a_send[...] = (a_own[theirs, :] + a_in[theirs, :].astype(F32)).astype(BF)
    b_own[...] = b_keep[:128, :] + b_in[:128, :].astype(F32)
    b_send[...] = (b_keep[128:, :] + b_in[128:, :].astype(F32)).astype(BF)


def reduce_second_kernel(sc, a_keep, a_in, b_own, b_in, keep, *sends):
    rows, wide = keep.shape[0], a_keep.shape[1]
    for m in range(4):
        at = pl.ds(pl.multiple_of((sc[9] ^ m) * rows, rows), rows)
        left = a_keep[at, :] + a_in[at, :].astype(F32)
        right = b_own[at, :] + b_in[at, :].astype(F32)
        target = keep if m == 0 else sends[m - 1]
        target[:, :wide] = left.astype(target.dtype)
        target[:, wide:] = right.astype(target.dtype)


def place_rows_kernel(sc, *refs):
    size = refs[0].shape[0]
    for m in range(len(refs) - 1):
        refs[-1][pl.ds(pl.multiple_of((sc[9] ^ m) * size, size), size), :] = refs[m][...]


def place_final_kernel(sc, *refs):
    @pl.when(pl.program_id(0) == sc[10])
    def _():
        refs[-1][...] = refs[-3][...].astype(F32)

    @pl.when(pl.program_id(0) != sc[10])
    def _():
        refs[-1][...] = refs[-2][...].astype(F32)


def on_device(query_in, key_in, value_in, grad_out, out_weight):
    clips, tile_rows, tile_cols, tile, feats = query_in.shape
    model = grad_out.shape[-1]
    head = feats // HEADS
    scale = head**-0.5
    assert (clips, tile_rows, tile_cols) == (1, 1, 1) and lax.axis_size("wa") == HEADS
    dp_size, ha_size = lax.axis_size("dp"), lax.axis_size("ha")
    fast = dp_size == 2 and ha_size == 4
    d, w = lax.axis_index("dp"), lax.axis_index("wa")
    core = w & 1
    q2, k2, v2 = (a.reshape(tile, feats) for a in (query_in, key_in, value_in))
    g2 = grad_out.reshape(tile, model)
    half = model // 2

    def across(value):
        return xor_send(value, "wa", 2)

    def partner(value):
        return xor_send(value, "wa", 1)

    if fast:
        w_own = out_weight
        swap = [(HEADS * i + j, HEADS * (1 - i) + j) for i in range(2) for j in range(0, HEADS, 2)]
        w_even = lax.ppermute(out_weight, ("dp", "wa"), swap)
        w_odd = lax.ppermute(w_even, "wa", [(j, j + 1) for j in range(0, HEADS, 2)])
    else:
        whole = lax.all_gather(out_weight, "dp", axis=0, tiled=True)
        w_own, w_even = whole[: 2 * head], whole[2 * head :]
        w_odd = w_even

    kv_near, kv_far, q_near, q_far = call(
        pack_kernel, [q2, k2, v2], [sds((2, 2, tile, head), BF)] * 2 + [sds((2, tile, head), BF)] * 2
    )

    def gather(near, far):
        return [near, partner(near), far, partner(far)]

    kv_far = across(kv_far)
    q_far = across(q_far)
    kv = gather(kv_near, kv_far)
    qs = gather(q_near, q_far)
    above = gather(step_send(kv_near, "ha", 1), step_send(kv_far, "ha", 1))
    below = gather(step_send(kv_near, "ha", -1), step_send(kv_far, "ha", -1))

    def piece_specs(pieces):
        return [
            pl.BlockSpec((1,) + a.shape[1:], lambda *_, i=i, n=a.ndim: (i % 2,) + (0,) * (n - 1))
            for i, a in enumerate(pieces)
        ]

    steps = 4
    chunk = model // steps
    do_near, do_far = call(
        grad_attn_kernel,
        [g2, w_own, w_even, w_odd],
        [sds((2, tile, head), BF)] * 2,
        grid=(steps,),
        in_specs=[pl.BlockSpec((a.shape[0], chunk), lambda i: (0, i)) for a in (g2, w_own, w_even, w_odd)],
        scratch=[pltpu.VMEM((tile, feats), F32), pltpu.VMEM((4, tile, head), BF), pltpu.VMEM((feats, chunk), BF)],
        flops=2 * tile * model * feats,
    )
    dos = gather(do_near, across(do_far))

    pair = 2 * 30 * tile * tile * head

    def by_tile(*shape):
        return pl.BlockSpec((1,) + shape, lambda b: (b,) + (0,) * len(shape))

    halo = above + kv + below
    att_near, att_far, att_b, inv_b, probs = call(
        lambda *a: forward_kernel(scale * math.log2(math.e), *a),
        qs + halo,
        [sds((2, tile, head), BF)] * 2
        + [sds((4, tile, head), BF), sds((4, tile, head), F32), sds((4, 3, tile, 3 * tile), BF)],
        grid=(4,),
        in_specs=piece_specs(qs + halo),
        out_specs=[None] * 2 + [by_tile(tile, head), by_tile(tile, head), by_tile(3, tile, 3 * tile)],
        scratch=[
            pltpu.VMEM((3, 4 * tile, head), BF),
            pltpu.VMEM((3, 4 * tile, 2 * head), BF),
            pltpu.VMEM((4 * tile, head), BF),
            pltpu.VMEM((3, tile, 3 * tile), F32),
            pltpu.VMEM((tile, 128), F32),
            pltpu.VMEM((tile, 2 * head), F32),
        ],
        flops=2 * pair,
        exps=30 * tile * tile,
    )
    atts = gather(att_near, across(att_far))
    near, p_near, far, p_far = atts

    def back(row, extra):
        pieces = qs + (above, kv, below)[row] + dos
        p_spec = pl.BlockSpec((1, 1, tile, 3 * tile), lambda b: (b, row, 0, 0))
        if row == 1:
            outs = [sds((2, tile, head), BF)] * 2 + [sds((2, 4 * tile, head), F32)]
            out_specs = [None] * 3
        else:
            outs = [sds((4, tile, head), F32), sds((2, 4 * tile, head), BF)]
            out_specs = [by_tile(tile, head), None]
        return call(
            lambda *a: backward_kernel(row, scale, *a),
                pieces + [att_b, inv_b, probs] + extra,
            outs,
            grid=(4,),
            in_specs=piece_specs(pieces) + [by_tile(tile, head)] * 2 + [p_spec] + [by_tile(tile, head)] * len(extra),
            out_specs=out_specs,
            scratch=[pltpu.VMEM((4 * tile, head), BF)] * 4
            + [pltpu.VMEM((head, 4 * tile), F32)] * 2
            + [pltpu.VMEM((tile, head), F32)],
            flops=4 * pair // 3,
        )

    dq_part, dkv_up = back(0, [])
    dq_part, dkv_down = back(2, [dq_part])
    dq_near, dq_far, dkv_own = back(1, [dq_part])
    from_below = step_send(dkv_up, "ha", -1)
    from_above = step_send(dkv_down, "ha", 1)
    dqs = gather(dq_near, across(dq_far))
    dkv_near, dkv_far = call(combine_kernel, [dkv_own, from_above, from_below], [sds((2, 2, tile, head), BF)] * 2)
    dkvs = gather(dkv_near, across(dkv_far))
    query_grad, key_grad, value_grad = call(
        finish_kernel, dqs + dkvs, [sds((tile, feats), F32)] * 3,
        in_specs=piece_specs(dqs + dkvs),
    )

    def cols(a, n):
        return pl.BlockSpec((a.shape[0], n), lambda i: (0, i))

    (outcome,) = call(
        outcome_kernel,
        atts + [w_own, w_even, w_odd],
        [sds((tile, model), BF)],
        grid=(steps,),
        in_specs=piece_specs(atts) + [cols(a, chunk) for a in (w_own, w_even, w_odd)],
        out_specs=[pl.BlockSpec((tile, chunk), lambda i: (0, i))],
        scratch=[pltpu.VMEM((4, tile, head), BF), pltpu.VMEM((tile, feats), BF), pltpu.VMEM((feats, chunk), BF)],
        flops=2 * tile * model * feats,
    )
    if fast:
        g_mine = lax.dynamic_slice_in_dim(g2, core * half, half, 1)
        g_other = partner(lax.dynamic_slice_in_dim(g2, (1 - core) * half, half, 1))
        share, wide = feats // 2, half // 2
        a_own, a_send, b_keep, b_send = call(
            weight_kernel,
                [near, far, p_near, p_far, g_mine, g_other],
            [sds((share, wide), F32), sds((share, wide), BF)] * 2,
            grid=(2,),
            in_specs=[None] * 4 + [cols(g_mine, wide), cols(g_other, wide)],
            scratch=[
                pltpu.VMEM((4, 2 * tile, head), BF),
                pltpu.VMEM((feats, 2 * tile), BF),
                pltpu.VMEM((2 * tile, wide), BF),
                pltpu.VMEM((feats, wide), F32),
            ],
            flops=4 * tile * feats * half,
        )
        a_in = xor_send(a_send, "dp", 1)
        b_in = across(b_send)
        a_own, a_send, b_keep, b_send = call(
            reduce_first_kernel,
                [a_own, a_in, b_keep, b_in],
            [sds((share // 2, wide), F32), sds((share // 2, wide), BF)] * 2,
        )
        a_in = across(a_send)
        b_in = xor_send(b_send, "dp", 1)
        rows = share // 8
        keep, *sends = call(
            reduce_second_kernel, [a_own, a_in, b_keep, b_in], [sds((rows, half), F32)] + [sds((rows, half), BF)] * 3
        )
        got = [xor_send(sends[m - 1], "ha", m) for m in (1, 2, 3)]
        piece = (keep + got[0].astype(F32) + got[1].astype(F32) + got[2].astype(F32)).astype(BF)
        pieces = [piece] + [xor_send(piece, "ha", m) for m in (1, 2, 3)]
        (piece,) = call(place_rows_kernel, pieces, [sds((4 * rows, half), BF)])
        other = across(piece)

        def rows_of(flip):
            return pl.BlockSpec((share // 2, half), lambda j: ((lax.axis_index("wa") >> 1) ^ flip, j))

        (begun,) = call(
            place_final_kernel, [piece, partner(piece)], [sds((share, model), F32)], grid=(2,), out_specs=[rows_of(0)]
        )
        (weight_grad,) = call(
            place_final_kernel,
            [begun, other, partner(other)],
            [sds((share, model), F32)],
            grid=(2,),
            in_specs=[pl.BlockSpec(memory_space=pl.ANY), None, None],
            out_specs=[rows_of(1)],
            alias={0: 0},
        )
    else:
        att = jnp.zeros((tile, feats), BF)
        for m, value in enumerate((near[0], p_near[1], far[0], p_far[1])):
            att = lax.dynamic_update_slice_in_dim(att, value, (w ^ m) * head, 1)
        local = dot(att, g2, TN)
        summed = lax.psum(local, ("dp", "ha", "wa"))
        weight_grad = lax.dynamic_slice_in_dim(summed, d * (feats // dp_size), feats // dp_size, 0)
    return (
        outcome.reshape(grad_out.shape),
        query_grad.reshape(query_in.shape),
        key_grad.reshape(query_in.shape),
        value_grad.reshape(query_in.shape),
        weight_grad,
    )


def solution(mesh):
    tiles = P("dp", "ha", "wa", None, None)
    return jax.shard_map(
        on_device,
        mesh=mesh,
        in_specs=(tiles, tiles, tiles, tiles, P("dp", None)),
        out_specs=(tiles, tiles, tiles, tiles, P("dp", None)),
        check_vma=False,
    )
```

profile of v0, /device:TPU:0, one launch (start us, length us, event | category | flops | bytes accessed | tf_op | source)
XLA Modules:
  0.0 195.3 jit_solution(4962803847036482075)
XLA Ops:
  0.6 4.9 %collective-permute-start.17 = (bf16[256,3072]{1,0:T(8,128)(2,1)}, bf16[256,3072]{1,0:T(8,128)(2,1)S(1)}, u32[]{:S(2)}, u32[]{:S(2)}) collective-permute-start(bf16[256,3072]{1,0:T(8,128)(2,1)} %refs_1_.1), channel_id=1, source_target_pairs={{0,16},{2,18},{16,0},{18,2},{4,20},{6,22},{20,4},{22,6},{8,24},{10... | collective-permute-start | bytes 4718600 | tf_op jit(solution)/shard_map/ppermute | solution.py:373
  9.5 4.4 %collective-permute-done.1.refs_2_ = bf16[2,384,128]{2,1,0:T(8,128)(2,1)S(1)} collective-permute-done((bf16[2,384,128]{2,1,0:T(8,128)(2,1)}, bf16[2,384,128]{2,1,0:T(8,128)(2,1)S(1)}, u32[]{:S(2)}, u32[]{:S(2)}) %collective-permute-start.1) | collective-permute-done | bytes 196640 | tf_op jit(solution)/shard_map/ppermute | solution.py:18
  13.8 3.5 %collective-permute-start.3 = (bf16[2,2,384,128]{3,2,1,0:T(8,128)(2,1)}, bf16[2,2,384,128]{3,2,1,0:T(8,128)(2,1)S(1)}, u32[]{:S(2)}, u32[]{:S(2)}) collective-permute-start(bf16[2,2,384,128]{3,2,1,0:T(8,128)(2,1)} %get-tuple-element.42.refs_8_.refs_4_), channel_id=1, source_target_pairs={{0,4},{4,8},{8,12},{1,5},{5,9},{9,13},{2,6},{6,10},{10,14},{3,7},{... | collective-permute-start | bytes 1179656 | tf_op jit(solution)/shard_map/ppermute | solution.py:24
  20.3 6.4 %collective-permute-done.3.refs_4_ = bf16[2,2,384,128]{3,2,1,0:T(8,128)(2,1)S(1)} collective-permute-done((bf16[2,2,384,128]{3,2,1,0:T(8,128)(2,1)}, bf16[2,2,384,128]{3,2,1,0:T(8,128)(2,1)S(1)}, u32[]{:S(2)}, u32[]{:S(2)}) %collective-permute-start.3) | collective-permute-done | bytes 393248 | tf_op jit(solution)/shard_map/ppermute | solution.py:24
  28.9 3.5 %collective-permute-start.6 = (bf16[2,2,384,128]{3,2,1,0:T(8,128)(2,1)S(1)}, bf16[2,2,384,128]{3,2,1,0:T(8,128)(2,1)S(1)}, u32[]{:S(2)}, u32[]{:S(2)}) collective-permute-start(bf16[2,2,384,128]{3,2,1,0:T(8,128)(2,1)S(1)} %collective-permute-done.5.refs_10_.refs_6_), channel_id=1, source_target_pairs={{0,4},{4,8},{8,12},{1,5},{5,9},{9,13},{2,6},{6,10},{10,14},{3,7},{... | collective-permute-start | bytes 1179656 | tf_op jit(solution)/shard_map/ppermute | solution.py:24
  36.3 2.8 %dynamic-slice_bitcast_fusion = (bf16[384,1536]{1,0:T(8,128)(2,1)S(1)}, bf16[384,1536]{1,0:T(8,128)(2,1)}) fusion(bf16[1,1,1,384,3072]{4,3,2,1,0:T(8,128)(2,1)} %param.8, s32[]{:T(128)S(6)} %select_n.7, s32[]{:T(128)S(6)} %select_n.6), kind=kLoop, calls=%fused_computation | loop fusion | bytes 4718600 | tf_op jit(solution)/shard_map/dynamic_slice | solution.py:491
  40.8 5.0 %collective-permute-done.12.refs_14_.refs_6_ = bf16[2,2,384,128]{3,2,1,0:T(8,128)(2,1)S(1)} collective-permute-done((bf16[2,2,384,128]{3,2,1,0:T(8,128)(2,1)S(1)}, bf16[2,2,384,128]{3,2,1,0:T(8,128)(2,1)S(1)}, u32[]{:S(2)}, u32[]{:S(2)}) %collective-permute-start.12) | collective-permute-done | bytes 393248 | tf_op jit(solution)/shard_map/ppermute | solution.py:24
  48.4 11.0 %shard_map.93 = (bf16[2,384,128]{2,1,0:T(8,128)(2,1)}, bf16[2,384,128]{2,1,0:T(8,128)(2,1)}, bf16[4,384,128]{2,1,0:T(8,128)(2,1)}, f32[4,384,128]{2,1,0:T(8,128)}, bf16[4,3,384,1152]{3,2,1,0:T(8,128)(2,1)}) custom-call(bf16[2,384,128]{2,1,0:T(8,128)(2,1)} %get-tuple-element.40.refs_0_, bf16[2,384,128]{2,1,0:T(8,128)(2,1)} %copy-done.3, ...), custom_call_target="tpu_custom_call" | custom-call | flops 2264924160 | bytes 17694720 | tf_op jit(solution)/shard_map/pallas_call | solution.py:51
  60.9 5.6 %collective-permute-done.15.refs_2_.refs_1_ = bf16[2,384,128]{2,1,0:T(8,128)(2,1)S(1)} collective-permute-done((bf16[2,384,128]{2,1,0:T(8,128)(2,1)}, bf16[2,384,128]{2,1,0:T(8,128)(2,1)S(1)}, u32[]{:S(2)}, u32[]{:S(2)}) %collective-permute-start.15) | collective-permute-done | bytes 196640 | tf_op jit(solution)/shard_map/ppermute | solution.py:18
  68.6 5.0 %shard_map.101 = (f32[256,768]{1,0:T(8,128)}, bf16[256,768]{1,0:T(8,128)(2,1)}, f32[256,768]{1,0:T(8,128)}, bf16[256,768]{1,0:T(8,128)(2,1)}) custom-call(bf16[2,384,128]{2,1,0:T(8,128)(2,1)} %get-tuple-element.44.refs_0_, bf16[2,384,128]{2,1,0:T(8,128)(2,1)} %copy-done.37, bf16[2,384,128]{2,1,0:T(8,128)(2,1)} %copy-done.38, ...), custom_call_target="tpu_custom_call" | custom-call | flops 1207959552 | bytes 5505024 | tf_op jit(solution)/shard_map/pallas_call | solution.py:51
  76.9 5.8 %shard_map.95 = (bf16[2,384,128]{2,1,0:T(8,128)(2,1)}, bf16[2,384,128]{2,1,0:T(8,128)(2,1)}) custom-call(bf16[384,3072]{1,0:T(8,128)(2,1)} %bitcast.12, bf16[256,3072]{1,0:T(8,128)(2,1)} %refs_1_.1, bf16[256,3072]{1,0:T(8,128)(2,1)} %copy-done, bf16[256,3072]{1,0:T(8,128)(2,1)} %copy-done.1), custom_call_target="tpu_custom_call" | custom-call | flops 1207959552 | bytes 7471104 | tf_op jit(solution)/shard_map/pallas_call | solution.py:51
  86.3 2.7 %shard_map.102 = (f32[128,768]{1,0:T(8,128)}, bf16[128,768]{1,0:T(8,128)(2,1)}, f32[128,768]{1,0:T(8,128)}, bf16[128,768]{1,0:T(8,128)(2,1)}) custom-call(f32[256,768]{1,0:T(8,128)} %get-tuple-element.63.refs_0_, bf16[256,768]{1,0:T(8,128)(2,1)} %copy-done.17, f32[256,768]{1,0:T(8,128)} %get-tuple-element.65.refs_2_, bf16[256,768]{1,0:T(8,128)(2,1)} %copy-done.18), custom_call_target="tpu_custom_call" | custom-call | bytes 3538944 | tf_op jit(solution)/shard_map/pallas_call | solution.py:51
  100.0 6.0 %collective-permute-start.36 = (bf16[32,1536]{1,0:T(8,128)(2,1)}, bf16[32,1536]{1,0:T(8,128)(2,1)S(1)}, u32[]{:S(2)}, u32[]{:S(2)}) collective-permute-start(bf16[32,1536]{1,0:T(8,128)(2,1)} %get-tuple-element.73), channel_id=1, source_target_pairs={{0,8},{4,12},{8,0},{12,4},{1,9},{5,13},{9,1},{13,5},{2,10},{6,14},... | collective-permute-start | bytes 294920 | tf_op jit(solution)/shard_map/ppermute | solution.py:18
  106.7 5.6 %shard_map.96 = (f32[4,384,128]{2,1,0:T(8,128)}, bf16[2,1536,128]{2,1,0:T(8,128)(2,1)}) custom-call(bf16[2,384,128]{2,1,0:T(8,128)(2,1)} %get-tuple-element.40.refs_0_, bf16[2,384,128]{2,1,0:T(8,128)(2,1)} %copy-done.3, bf16[2,384,128]{2,1,0:T(8,128)(2,1)} %copy-done.2, bf16[2,384,128]{2,1,0:T(8,128)(2,1)} %copy-done.4, bf16[2,2,384,128]{3,2,1,0:T(8,128)(2,1)} %copy-done.23, ...), custom_call_target="tpu_custom_call" | custom-call | flops 1509949440 | bytes 16515072 | tf_op jit(solution)/shard_map/pallas_call | solution.py:51
  112.4 8.0 %shard_map.97 = (f32[4,384,128]{2,1,0:T(8,128)}, bf16[2,1536,128]{2,1,0:T(8,128)(2,1)}) custom-call(bf16[2,384,128]{2,1,0:T(8,128)(2,1)} %get-tuple-element.40.refs_0_, bf16[2,384,128]{2,1,0:T(8,128)(2,1)} %copy-done.3, bf16[2,384,128]{2,1,0:T(8,128)(2,1)} %copy-done.2, bf16[2,384,128]{2,1,0:T(8,128)(2,1)} %copy-done.4, ...), custom_call_target="tpu_custom_call" | custom-call | flops 1509949440 | bytes 17301504 | tf_op jit(solution)/shard_map/pallas_call | solution.py:51
  120.4 6.0 %collective-permute-start.25 = (bf16[2,1536,128]{2,1,0:T(8,128)(2,1)}, bf16[2,1536,128]{2,1,0:T(8,128)(2,1)S(1)}, u32[]{:S(2)}, u32[]{:S(2)}) collective-permute-start(bf16[2,1536,128]{2,1,0:T(8,128)(2,1)} %get-tuple-element.56), channel_id=1, source_target_pairs={{0,4},{4,8},{8,12},{1,5},{5,9},{9,13},{2,6},{6,10},{10,14},{3,7},{... | collective-permute-start | bytes 2359304 | tf_op jit(solution)/shard_map/ppermute | solution.py:24
  127.9 2.7 %collective-permute-start.38 = (bf16[32,1536]{1,0:T(8,128)(2,1)S(1)}, bf16[32,1536]{1,0:T(8,128)(2,1)S(1)}, u32[]{:S(2)}, u32[]{:S(2)}) collective-permute-start(bf16[32,1536]{1,0:T(8,128)(2,1)S(1)} %add_convert_fusion.refs_0_), channel_id=1, source_target_pairs={{0,4},{4,0},{8,12},{12,8},{1,5},{5,1},{9,13},{13,9},{2,6},{6,2},{1... | collective-permute-start | bytes 294920 | tf_op jit(solution)/shard_map/ppermute | solution.py:18
  133.0 14.8 %collective-permute-done.38.refs_1_ = bf16[32,1536]{1,0:T(8,128)(2,1)S(1)} collective-permute-done((bf16[32,1536]{1,0:T(8,128)(2,1)S(1)}, bf16[32,1536]{1,0:T(8,128)(2,1)S(1)}, u32[]{:S(2)}, u32[]{:S(2)}) %collective-permute-start.38) | collective-permute-done | bytes 98336 | tf_op jit(solution)/shard_map/ppermute | solution.py:18
  147.8 2.8 %collective-permute-done.39.refs_2_ = bf16[32,1536]{1,0:T(8,128)(2,1)S(1)} collective-permute-done((bf16[32,1536]{1,0:T(8,128)(2,1)S(1)}, bf16[32,1536]{1,0:T(8,128)(2,1)S(1)}, u32[]{:S(2)}, u32[]{:S(2)}) %collective-permute-start.39) | collective-permute-done | bytes 98336 | tf_op jit(solution)/shard_map/ppermute | solution.py:18
  154.9 8.3 %shard_map.98 = (bf16[2,384,128]{2,1,0:T(8,128)(2,1)}, bf16[2,384,128]{2,1,0:T(8,128)(2,1)}, f32[2,1536,128]{2,1,0:T(8,128)}) custom-call(bf16[2,384,128]{2,1,0:T(8,128)(2,1)} %get-tuple-element.40.refs_0_, bf16[2,384,128]{2,1,0:T(8,128)(2,1)} %copy-done.3, bf16[2,384,128]{2,1,0:T(8,128)(2,1)} %copy-done.2, bf16[2,384,128]{2,1,0:T(8,128)(2,1)} %copy-done.4, ...), custom_call_target="tpu_custom_call" | custom-call | flops 1509949440 | bytes 17694720 | tf_op jit(solution)/shard_map/pallas_call | solution.py:51
  164.3 3.0 %shard_map.99 = (bf16[2,2,384,128]{3,2,1,0:T(8,128)(2,1)}, bf16[2,2,384,128]{3,2,1,0:T(8,128)(2,1)}) custom-call(f32[2,1536,128]{2,1,0:T(8,128)} %get-tuple-element.55.refs_0_, bf16[2,1536,128]{2,1,0:T(8,128)(2,1)} %copy-done.10, bf16[2,1536,128]{2,1,0:T(8,128)(2,1)} %copy-done.11), custom_call_target="tpu_custom_call" | custom-call | bytes 3932160 | tf_op jit(solution)/shard_map/pallas_call | solution.py:51
  169.8 7.5 %collective-permute-done.28.refs_6_ = bf16[2,2,384,128]{3,2,1,0:T(8,128)(2,1)S(1)} collective-permute-done((bf16[2,2,384,128]{3,2,1,0:T(8,128)(2,1)}, bf16[2,2,384,128]{3,2,1,0:T(8,128)(2,1)S(1)}, u32[]{:S(2)}, u32[]{:S(2)}) %collective-permute-start.28) | collective-permute-done | bytes 393248 | tf_op jit(solution)/shard_map/ppermute | solution.py:18
  181.9 5.7 %shard_map.94 = bf16[384,3072]{1,0:T(8,128)(2,1)} custom-call(bf16[2,384,128]{2,1,0:T(8,128)(2,1)} %get-tuple-element.44.refs_0_, bf16[2,384,128]{2,1,0:T(8,128)(2,1)} %copy-done.38, bf16[2,384,128]{2,1,0:T(8,128)(2,1)} %copy-done.37, bf16[2,384,128]{2,1,0:T(8,128)(2,1)} %copy-done.39, bf16[256,3072]{1,0:T(8,128)(2,1)} %refs_1_.1, ...), custom_call_target="tpu_custom_call" | custom-call | flops 1207959552 | bytes 7864320 | tf_op jit(solution)/shard_map/pallas_call | solution.py:51
  192.3 3.0 %shard_map.100 = (f32[384,512]{1,0:T(8,128)}, f32[384,512]{1,0:T(8,128)}, f32[384,512]{1,0:T(8,128)}) custom-call(bf16[2,384,128]{2,1,0:T(8,128)(2,1)} %get-tuple-element.53.refs_0_, bf16[2,384,128]{2,1,0:T(8,128)(2,1)} %copy-done.32, bf16[2,384,128]{2,1,0:T(8,128)(2,1)} %copy-done.31, bf16[2,384,128]{2,1,0:T(8,128)(2,1)} %copy-done.33, ...), custom_call_target="tpu_custom_call" | custom-call | bytes 4718592 | tf_op jit(solution)/shard_map/pallas_call | solution.py:51
  (171 shorter events, 60.2 us)
Async XLA Ops:
  0.6 33.3 %collective-permute-start.17 = (bf16[256,3072]{1,0:T(8,128)(2,1)}, bf16[256,3072]{1,0:T(8,128)(2,1)S(1)}, u32[]{:S(2)}, u32[]{:S(2)}) collective-permute-start(bf16[256,3072]{1,0:T(8,128)(2,1)} %refs_1_.1), channel_id=1, source_target_pairs={{0,16},{2,18},{16,0},{18,2},{4,20},{6,22},{20,4},{22,6},{8,24},{10... | collective-permute-start | bytes 4718600 | tf_op jit(solution)/shard_map/ppermute | solution.py:373
  13.8 12.8 %collective-permute-start.3 = (bf16[2,2,384,128]{3,2,1,0:T(8,128)(2,1)}, bf16[2,2,384,128]{3,2,1,0:T(8,128)(2,1)S(1)}, u32[]{:S(2)}, u32[]{:S(2)}) collective-permute-start(bf16[2,2,384,128]{3,2,1,0:T(8,128)(2,1)} %get-tuple-element.42.refs_8_.refs_4_), channel_id=1, source_target_pairs={{0,4},{4,8},{8,12},{1,5},{5,9},{9,13},{2,6},{6,10},{10,14},{3,7},{... | collective-permute-start | bytes 1179656 | tf_op jit(solution)/shard_map/ppermute | solution.py:24
  17.3 11.5 %collective-permute-start.5 = (bf16[2,2,384,128]{3,2,1,0:T(8,128)(2,1)}, bf16[2,2,384,128]{3,2,1,0:T(8,128)(2,1)S(1)}, u32[]{:S(2)}, u32[]{:S(2)}) collective-permute-start(bf16[2,2,384,128]{3,2,1,0:T(8,128)(2,1)} %get-tuple-element.43), channel_id=1, source_target_pairs={{0,2},{1,3},{2,0},{3,1},{4,6},{5,7},{6,4},{7,5},{8,10},{9,11},{10,... | collective-permute-start | bytes 1179656 | tf_op jit(solution)/shard_map/ppermute | solution.py:18
  18.9 13.4 %collective-permute-start.8 = (bf16[2,2,384,128]{3,2,1,0:T(8,128)(2,1)}, bf16[2,2,384,128]{3,2,1,0:T(8,128)(2,1)S(1)}, u32[]{:S(2)}, u32[]{:S(2)}) collective-permute-start(bf16[2,2,384,128]{3,2,1,0:T(8,128)(2,1)} %get-tuple-element.42.refs_8_.refs_4_), channel_id=1, source_target_pairs={{0,1},{1,0},{2,3},{3,2},{4,5},{5,4},{6,7},{7,6},{8,9},{9,8},{10,11... | collective-permute-start | bytes 1179656 | tf_op jit(solution)/shard_map/ppermute | solution.py:18
  19.0 13.7 %collective-permute-start.10 = (bf16[2,2,384,128]{3,2,1,0:T(8,128)(2,1)}, bf16[2,2,384,128]{3,2,1,0:T(8,128)(2,1)}, u32[]{:S(2)}, u32[]{:S(2)}) collective-permute-start(bf16[2,2,384,128]{3,2,1,0:T(8,128)(2,1)} %get-tuple-element.42.refs_8_.refs_4_), channel_id=1, source_target_pairs={{4,0},{8,4},{12,8},{5,1},{9,5},{13,9},{6,2},{10,6},{14,10},{7,3},{... | collective-permute-start | bytes 1179656 | tf_op jit(solution)/shard_map/ppermute | solution.py:24
  26.7 12.5 %collective-permute-start.4 = (bf16[2,2,384,128]{3,2,1,0:T(8,128)(2,1)S(1)}, bf16[2,2,384,128]{3,2,1,0:T(8,128)(2,1)}, u32[]{:S(2)}, u32[]{:S(2)}) collective-permute-start(bf16[2,2,384,128]{3,2,1,0:T(8,128)(2,1)S(1)} %collective-permute-done.3.refs_4_), channel_id=1, source_target_pairs={{0,1},{1,0},{2,3},{3,2},{4,5},{5,4},{6,7},{7,6},{8,9},{9,8},{10,11... | collective-permute-start | bytes 1179656 | tf_op jit(solution)/shard_map/ppermute | solution.py:18
  32.7 13.2 %collective-permute-start.12 = (bf16[2,2,384,128]{3,2,1,0:T(8,128)(2,1)S(1)}, bf16[2,2,384,128]{3,2,1,0:T(8,128)(2,1)S(1)}, u32[]{:S(2)}, u32[]{:S(2)}) collective-permute-start(bf16[2,2,384,128]{3,2,1,0:T(8,128)(2,1)S(1)} %collective-permute-done.5.refs_10_.refs_6_), channel_id=1, source_target_pairs={{4,0},{8,4},{12,8},{5,1},{9,5},{13,9},{6,2},{10,6},{14,10},{7,3},{... | collective-permute-start | bytes 1179656 | tf_op jit(solution)/shard_map/ppermute | solution.py:24
  34.0 41.7 %collective-permute-start.18 = (bf16[256,3072]{1,0:T(8,128)(2,1)S(1)}, bf16[256,3072]{1,0:T(8,128)(2,1)S(1)}, u32[]{:S(2)}, u32[]{:S(2)}) collective-permute-start(bf16[256,3072]{1,0:T(8,128)(2,1)S(1)} %collective-permute-done.17.refs_5_.refs_2_), channel_id=1, source_target_pairs={{0,1},{2,3},{4,5},{6,7},{8,9},{10,11},{12,13},{14,15},{16,17},{18,... | collective-permute-start | bytes 4718600 | tf_op jit(solution)/shard_map/ppermute | solution.py:374
  39.1 27.4 %collective-permute-start.30 = (bf16[384,1536]{1,0:T(8,128)(2,1)S(1)}, bf16[384,1536]{1,0:T(8,128)(2,1)}, u32[]{:S(2)}, u32[]{:S(2)}) collective-permute-start(bf16[384,1536]{1,0:T(8,128)(2,1)S(1)} %get-tuple-element.75), channel_id=1, source_target_pairs={{0,1},{1,0},{2,3},{3,2},{4,5},{5,4},{6,7},{7,6},{8,9},{9,8},{10,11... | collective-permute-start | bytes 3538952 | tf_op jit(solution)/shard_map/ppermute | solution.py:18
  92.8 13.2 %collective-permute-start.19 = (bf16[2,384,128]{2,1,0:T(8,128)(2,1)S(1)}, bf16[2,384,128]{2,1,0:T(8,128)(2,1)S(1)}, u32[]{:S(2)}, u32[]{:S(2)}) collective-permute-start(bf16[2,384,128]{2,1,0:T(8,128)(2,1)S(1)} %copy-done.5), channel_id=1, source_target_pairs={{0,1},{1,0},{2,3},{3,2},{4,5},{5,4},{6,7},{7,6},{8,9},{9,8},{10,11... | collective-permute-start | bytes 589832 | tf_op jit(solution)/shard_map/ppermute | solution.py:18
  92.9 13.1 %collective-permute-start.21 = (bf16[2,384,128]{2,1,0:T(8,128)(2,1)S(1)}, bf16[2,384,128]{2,1,0:T(8,128)(2,1)S(1)}, u32[]{:S(2)}, u32[]{:S(2)}) collective-permute-start(bf16[2,384,128]{2,1,0:T(8,128)(2,1)S(1)} %collective-permute-done.20.refs_10_), channel_id=1, source_target_pairs={{0,1},{1,0},{2,3},{3,2},{4,5},{5,4},{6,7},{7,6},{8,9},{9,8},{10,11... | collective-permute-start | bytes 589832 | tf_op jit(solution)/shard_map/ppermute | solution.py:18
  100.0 27.8 %collective-permute-start.37 = (bf16[32,1536]{1,0:T(8,128)(2,1)}, bf16[32,1536]{1,0:T(8,128)(2,1)S(1)}, u32[]{:S(2)}, u32[]{:S(2)}) collective-permute-start(bf16[32,1536]{1,0:T(8,128)(2,1)} %get-tuple-element.74), channel_id=1, source_target_pairs={{0,12},{4,8},{8,4},{12,0},{1,13},{5,9},{9,5},{13,1},{2,14},{6,10},... | collective-permute-start | bytes 294920 | tf_op jit(solution)/shard_map/ppermute | solution.py:18
  100.0 27.8 %collective-permute-start.36 = (bf16[32,1536]{1,0:T(8,128)(2,1)}, bf16[32,1536]{1,0:T(8,128)(2,1)S(1)}, u32[]{:S(2)}, u32[]{:S(2)}) collective-permute-start(bf16[32,1536]{1,0:T(8,128)(2,1)} %get-tuple-element.73), channel_id=1, source_target_pairs={{0,8},{4,12},{8,0},{12,4},{1,9},{5,13},{9,1},{13,5},{2,10},{6,14},... | collective-permute-start | bytes 294920 | tf_op jit(solution)/shard_map/ppermute | solution.py:18
  106.0 21.8 %collective-permute-start.35 = (bf16[32,1536]{1,0:T(8,128)(2,1)}, bf16[32,1536]{1,0:T(8,128)(2,1)S(1)}, u32[]{:S(2)}, u32[]{:S(2)}) collective-permute-start(bf16[32,1536]{1,0:T(8,128)(2,1)} %get-tuple-element.72), channel_id=1, source_target_pairs={{0,4},{4,0},{8,12},{12,8},{1,5},{5,1},{9,13},{13,9},{2,6},{6,2},{1... | collective-permute-start | bytes 294920 | tf_op jit(solution)/shard_map/ppermute | solution.py:18
  120.4 42.8 %collective-permute-start.25 = (bf16[2,1536,128]{2,1,0:T(8,128)(2,1)}, bf16[2,1536,128]{2,1,0:T(8,128)(2,1)S(1)}, u32[]{:S(2)}, u32[]{:S(2)}) collective-permute-start(bf16[2,1536,128]{2,1,0:T(8,128)(2,1)} %get-tuple-element.56), channel_id=1, source_target_pairs={{0,4},{4,8},{8,12},{1,5},{5,9},{9,13},{2,6},{6,10},{10,14},{3,7},{... | collective-permute-start | bytes 2359304 | tf_op jit(solution)/shard_map/ppermute | solution.py:24
  126.4 36.8 %collective-permute-start.26 = (bf16[2,1536,128]{2,1,0:T(8,128)(2,1)S(1)}, bf16[2,1536,128]{2,1,0:T(8,128)(2,1)S(1)}, u32[]{:S(2)}, u32[]{:S(2)}) collective-permute-start(bf16[2,1536,128]{2,1,0:T(8,128)(2,1)S(1)} %copy-done.43), channel_id=1, source_target_pairs={{4,0},{8,4},{12,8},{5,1},{9,5},{13,9},{6,2},{10,6},{14,10},{7,3},{... | collective-permute-start | bytes 2359304 | tf_op jit(solution)/shard_map/ppermute | solution.py:24
  127.9 19.9 %collective-permute-start.38 = (bf16[32,1536]{1,0:T(8,128)(2,1)S(1)}, bf16[32,1536]{1,0:T(8,128)(2,1)S(1)}, u32[]{:S(2)}, u32[]{:S(2)}) collective-permute-start(bf16[32,1536]{1,0:T(8,128)(2,1)S(1)} %add_convert_fusion.refs_0_), channel_id=1, source_target_pairs={{0,4},{4,0},{8,12},{12,8},{1,5},{5,1},{9,13},{13,9},{2,6},{6,2},{1... | collective-permute-start | bytes 294920 | tf_op jit(solution)/shard_map/ppermute | solution.py:18
  130.6 20.1 %collective-permute-start.39 = (bf16[32,1536]{1,0:T(8,128)(2,1)S(1)}, bf16[32,1536]{1,0:T(8,128)(2,1)S(1)}, u32[]{:S(2)}, u32[]{:S(2)}) collective-permute-start(bf16[32,1536]{1,0:T(8,128)(2,1)S(1)} %add_convert_fusion.refs_0_), channel_id=1, source_target_pairs={{0,8},{4,12},{8,0},{12,4},{1,9},{5,13},{9,1},{13,5},{2,10},{6,14},... | collective-permute-start | bytes 294920 | tf_op jit(solution)/shard_map/ppermute | solution.py:18
  130.6 20.1 %collective-permute-start.40 = (bf16[32,1536]{1,0:T(8,128)(2,1)S(1)}, bf16[32,1536]{1,0:T(8,128)(2,1)S(1)}, u32[]{:S(2)}, u32[]{:S(2)}) collective-permute-start(bf16[32,1536]{1,0:T(8,128)(2,1)S(1)} %add_convert_fusion.refs_0_), channel_id=1, source_target_pairs={{0,12},{4,8},{8,4},{12,0},{1,13},{5,9},{9,5},{13,1},{2,14},{6,10},... | collective-permute-start | bytes 294920 | tf_op jit(solution)/shard_map/ppermute | solution.py:18
  153.7 14.4 %collective-permute-start.42 = (bf16[128,1536]{1,0:T(8,128)(2,1)}, bf16[128,1536]{1,0:T(8,128)(2,1)S(1)}, u32[]{:S(2)}, u32[]{:S(2)}) collective-permute-start(bf16[128,1536]{1,0:T(8,128)(2,1)} %shard_map.104.refs_0_), channel_id=1, source_target_pairs={{0,2},{1,3},{2,0},{3,1},{4,6},{5,7},{6,4},{7,5},{8,10},{9,11},{10,... | collective-permute-start | bytes 1179656 | tf_op jit(solution)/shard_map/ppermute | solution.py:18
  168.2 19.4 %collective-permute-start.43 = (bf16[128,1536]{1,0:T(8,128)(2,1)S(1)}, bf16[128,1536]{1,0:T(8,128)(2,1)S(1)}, u32[]{:S(2)}, u32[]{:S(2)}) collective-permute-start(bf16[128,1536]{1,0:T(8,128)(2,1)S(1)} %collective-permute-done.42.refs_1_), channel_id=1, source_target_pairs={{0,1},{1,0},{2,3},{3,2},{4,5},{5,4},{6,7},{7,6},{8,9},{9,8},{10,11... | collective-permute-start | bytes 1179656 | tf_op jit(solution)/shard_map/ppermute | solution.py:18
  169.8 20.8 %collective-permute-start.27 = (bf16[2,2,384,128]{3,2,1,0:T(8,128)(2,1)}, bf16[2,2,384,128]{3,2,1,0:T(8,128)(2,1)S(1)}, u32[]{:S(2)}, u32[]{:S(2)}) collective-permute-start(bf16[2,2,384,128]{3,2,1,0:T(8,128)(2,1)} %get-tuple-element.58.refs_4_), channel_id=1, source_target_pairs={{0,1},{1,0},{2,3},{3,2},{4,5},{5,4},{6,7},{7,6},{8,9},{9,8},{10,11... | collective-permute-start | bytes 1179656 | tf_op jit(solution)/shard_map/ppermute | solution.py:18
  177.4 13.3 %collective-permute-start.29 = (bf16[2,2,384,128]{3,2,1,0:T(8,128)(2,1)S(1)}, bf16[2,2,384,128]{3,2,1,0:T(8,128)(2,1)S(1)}, u32[]{:S(2)}, u32[]{:S(2)}) collective-permute-start(bf16[2,2,384,128]{3,2,1,0:T(8,128)(2,1)S(1)} %collective-permute-done.28.refs_6_), channel_id=1, source_target_pairs={{0,1},{1,0},{2,3},{3,2},{4,5},{5,4},{6,7},{7,6},{8,9},{9,8},{10,11... | collective-permute-start | bytes 1179656 | tf_op jit(solution)/shard_map/ppermute | solution.py:18
  177.4 13.2 %collective-permute-start.22 = (bf16[2,384,128]{2,1,0:T(8,128)(2,1)S(1)}, bf16[2,384,128]{2,1,0:T(8,128)(2,1)S(1)}, u32[]{:S(2)}, u32[]{:S(2)}) collective-permute-start(bf16[2,384,128]{2,1,0:T(8,128)(2,1)S(1)} %copy-done.30), channel_id=1, source_target_pairs={{0,1},{1,0},{2,3},{3,2},{4,5},{5,4},{6,7},{7,6},{8,9},{9,8},{10,11... | collective-permute-start | bytes 589832 | tf_op jit(solution)/shard_map/ppermute | solution.py:18
  (65 other events, 413.5 us)
where the time goes:
time: 196 us; the launch traced here: 195 us
  Pallas kernels  69.1 us (35%)
  waiting for transfers between devices  61 us (31%)
  starting transfers between devices  51.6 us (26%)
  local copies, waits for them, and re-layouts  12.4 us (6%)
    pallas_call x15, Pallas kernels, call(): pl.pallas_call(lambda *refs: kernel(place_of(), *refs), out_shape=list(ou...  69.1 us
    ppermute x36, waiting for transfers between devices, xor_send(): return lax.ppermute(value, axis, [(i, i ^ mask) for i in range(count)])  48.2 us
    ppermute x36, starting transfers between devices, xor_send(): return lax.ppermute(value, axis, [(i, i ^ mask) for i in range(count)])  27.6 us
    ppermute x6, starting transfers between devices, step_send(): return lax.ppermute(value, axis, pairs)  16.8 us
    ppermute x6, waiting for transfers between devices, step_send(): return lax.ppermute(value, axis, pairs)  12.8 us
    unnamed x90, local copies, waits for them, and re-layouts  9.58 us
    ppermute x1, starting transfers between devices, on_device(): w_even = lax.ppermute(out_weight, ('dp', 'wa'), swap)  4.88 us
  transfers between devices with their start and end apart: 44, of which 17 were waited for; matrix products, arithmetic and copies ran while one was open for 1% of the time, Pallas kernels for 34%

commit v1 on v0

--- a/solution.py
+++ b/solution.py
@@ -86,32 +86,19 @@
             outs[2 + far][j] = q[:, cols]
 
 
-def stack_rows(core, own, even, odd, whole):
-    size = own.shape[0]
-    whole[:size, :] = own[...]
-
-    @pl.when(core == 0)
-    def _():
-        whole[size:, :] = even[...]
-
-    @pl.when(core == 1)
-    def _():
-        whole[size:, :] = odd[...]
-
-    return whole[...]
-
-
-def grad_attn_kernel(sc, g, w_own, w_even, w_odd, near, far, acc, by_head, whole):
+def grad_attn_kernel(sc, g, w_own, w_even, w_odd, near, far, acc, by_head):
     step = pl.program_id(0)
-    part = dot(g[...], stack_rows(sc[10], w_own, w_even, w_odd, whole), NT)
 
     @pl.when(step == 0)
     def _():
-        acc[...] = part
-
-    @pl.when(step > 0)
-    def _():
-        acc[...] += part
+        acc[...] = jnp.zeros_like(acc)
+
+    acc[:, :256] += dot(g[...], w_own[...], NT)
+    for core, rows in enumerate((w_even, w_odd)):
+
+        @pl.when(sc[10] == core)
+        def _():
+            acc[:, 256:] += dot(g[...], rows[...], NT)
 
     @pl.when(step == pl.num_programs(0) - 1)
     def _():
@@ -266,7 +253,7 @@
         dv[:, cols] = dkv_in[m][0, 1].astype(F32)
 
 
-def outcome_kernel(sc, near, p_near, far, p_far, w_own, w_even, w_odd, out, att, slots, whole):
+def outcome_kernel(sc, near, p_near, far, p_far, w_own, w_even, w_odd, out, att, slots):
     @pl.when(pl.program_id(0) == 0)
     def _():
         for m, piece in enumerate((near, p_near, far, p_far)):
@@ -274,7 +261,12 @@
         for slot in range(4):
             slots[:, slot * 128 : slot * 128 + 128] = att[sc[1 + slot]]
 
-    out[...] = dot(slots[...], stack_rows(sc[10], w_own, w_even, w_odd, whole), NN).astype(BF)
+    for core, rows in enumerate((w_even, w_odd)):
+
+        @pl.when(sc[10] == core)
+        def _():
+            total = dot(slots[:, :256], w_own[...], NN) + dot(slots[:, 256:], rows[...], NN)
+            out[...] = total.astype(BF)
 
 
 def weight_kernel(sc, near, far, p_near, p_far, g, g_other, a_own, a_send, b_keep, b_send, att, slots, both, res):
@@ -378,7 +370,9 @@
         w_odd = w_even
 
     kv_near, kv_far, q_near, q_far = call(
-        pack_kernel, [q2, k2, v2], [sds((2, 2, tile, head), BF)] * 2 + [sds((2, tile, head), BF)] * 2
+        pack_kernel,
+        [q2, k2, v2],
+        [sds((2, 2, tile, head), BF)] * 2 + [sds((2, tile, head), BF)] * 2,
     )
 
     def gather(near, far):
@@ -405,7 +399,7 @@
         [sds((2, tile, head), BF)] * 2,
         grid=(steps,),
         in_specs=[pl.BlockSpec((a.shape[0], chunk), lambda i: (0, i)) for a in (g2, w_own, w_even, w_odd)],
-        scratch=[pltpu.VMEM((tile, feats), F32), pltpu.VMEM((4, tile, head), BF), pltpu.VMEM((feats, chunk), BF)],
+        scratch=[pltpu.VMEM((tile, feats), F32), pltpu.VMEM((4, tile, head), BF)],
         flops=2 * tile * model * feats,
     )
     dos = gather(do_near, across(do_far))
@@ -466,7 +460,9 @@
     from_below = step_send(dkv_up, "ha", -1)
     from_above = step_send(dkv_down, "ha", 1)
     dqs = gather(dq_near, across(dq_far))
-    dkv_near, dkv_far = call(combine_kernel, [dkv_own, from_above, from_below], [sds((2, 2, tile, head), BF)] * 2)
+    dkv_near, dkv_far = call(
+        combine_kernel, [dkv_own, from_above, from_below], [sds((2, 2, tile, head), BF)] * 2
+    )
     dkvs = gather(dkv_near, across(dkv_far))
     query_grad, key_grad, value_grad = call(
         finish_kernel, dqs + dkvs, [sds((tile, feats), F32)] * 3,
@@ -483,7 +479,7 @@
         grid=(steps,),
         in_specs=piece_specs(atts) + [cols(a, chunk) for a in (w_own, w_even, w_odd)],
         out_specs=[pl.BlockSpec((tile, chunk), lambda i: (0, i))],
-        scratch=[pltpu.VMEM((4, tile, head), BF), pltpu.VMEM((tile, feats), BF), pltpu.VMEM((feats, chunk), BF)],
+        scratch=[pltpu.VMEM((4, tile, head), BF), pltpu.VMEM((tile, feats), BF)],
         flops=2 * tile * model * feats,
     )
     if fast:
@@ -510,12 +506,17 @@
             reduce_first_kernel,
                 [a_own, a_in, b_keep, b_in],
             [sds((share // 2, wide), F32), sds((share // 2, wide), BF)] * 2,
+            grid=(2,),
+            in_specs=[cols(a_own, wide // 2)] * 4,
+            out_specs=[pl.BlockSpec((share // 2, wide // 2), lambda i: (0, i))] * 4,
         )
         a_in = across(a_send)
         b_in = xor_send(b_send, "dp", 1)
         rows = share // 8
         keep, *sends = call(
-            reduce_second_kernel, [a_own, a_in, b_keep, b_in], [sds((rows, half), F32)] + [sds((rows, half), BF)] * 3
+            reduce_second_kernel,
+                [a_own, a_in, b_keep, b_in],
+            [sds((rows, half), F32)] + [sds((rows, half), BF)] * 3,
         )
         got = [xor_send(sends[m - 1], "ha", m) for m in (1, 2, 3)]
         piece = (keep + got[0].astype(F32) + got[1].astype(F32) + got[2].astype(F32)).astype(BF)
@@ -527,7 +528,11 @@
             return pl.BlockSpec((share // 2, half), lambda j: ((lax.axis_index("wa") >> 1) ^ flip, j))
 
         (begun,) = call(
-            place_final_kernel, [piece, partner(piece)], [sds((share, model), F32)], grid=(2,), out_specs=[rows_of(0)]
+            place_final_kernel,
+            [piece, partner(piece)],
+            [sds((share, model), F32)],
+            grid=(2,),
+            out_specs=[rows_of(0)],
         )
         (weight_grad,) = call(
             place_final_kernel,

time: 196 us -> 196 us (level)
  no operation moved by 1% of the time
where the time goes in v1:
time: 196 us; the launch traced here: 195 us
  Pallas kernels  69.1 us (35%)
  waiting for transfers between devices  60.8 us (31%)
  starting transfers between devices  51.6 us (26%)
  local copies, waits for them, and re-layouts  12.4 us (6%)
    pallas_call x15, Pallas kernels, call(): pl.pallas_call(lambda *refs: kernel(place_of(), *refs), out_shape=list(ou...  69.1 us
    ppermute x36, waiting for transfers between devices, xor_send(): return lax.ppermute(value, axis, [(i, i ^ mask) for i in range(count)])  48 us
    ppermute x36, starting transfers between devices, xor_send(): return lax.ppermute(value, axis, [(i, i ^ mask) for i in range(count)])  27.6 us
    ppermute x6, starting transfers between devices, step_send(): return lax.ppermute(value, axis, pairs)  16.8 us
    ppermute x6, waiting for transfers between devices, step_send(): return lax.ppermute(value, axis, pairs)  12.8 us
    unnamed x90, local copies, waits for them, and re-layouts  9.58 us
    ppermute x1, starting transfers between devices, on_device(): w_even = lax.ppermute(out_weight, ('dp', 'wa'), swap)  4.88 us
  transfers between devices with their start and end apart: 44, of which 17 were waited for; matrix products, arithmetic and copies ran while one was open for 1% of the time, Pallas kernels for 34%

profile of v1, /device:TPU:0, one launch (start us, length us, event | category | flops | bytes accessed | tf_op | source)
XLA Modules:
  0.0 195.1 jit_solution(7619914109445038131)
XLA Ops:
  0.6 4.9 %collective-permute-start.17 = (bf16[256,3072]{1,0:T(8,128)(2,1)}, bf16[256,3072]{1,0:T(8,128)(2,1)S(1)}, u32[]{:S(2)}, u32[]{:S(2)}) collective-permute-start(bf16[256,3072]{1,0:T(8,128)(2,1)} %refs_1_.1), channel_id=1, source_target_pairs={{0,16},{2,18},{16,0},{18,2},{4,20},{6,22},{20,4},{22,6},{8,24},{10... | collective-permute-start | bytes 4718600 | tf_op jit(solution)/shard_map/ppermute | solution.py:365
  9.5 4.4 %collective-permute-done.1.refs_2_ = bf16[2,384,128]{2,1,0:T(8,128)(2,1)S(1)} collective-permute-done((bf16[2,384,128]{2,1,0:T(8,128)(2,1)}, bf16[2,384,128]{2,1,0:T(8,128)(2,1)S(1)}, u32[]{:S(2)}, u32[]{:S(2)}) %collective-permute-start.1) | collective-permute-done | bytes 196640 | tf_op jit(solution)/shard_map/ppermute | solution.py:18
  13.8 3.5 %collective-permute-start.3 = (bf16[2,2,384,128]{3,2,1,0:T(8,128)(2,1)}, bf16[2,2,384,128]{3,2,1,0:T(8,128)(2,1)S(1)}, u32[]{:S(2)}, u32[]{:S(2)}) collective-permute-start(bf16[2,2,384,128]{3,2,1,0:T(8,128)(2,1)} %get-tuple-element.42.refs_8_.refs_4_), channel_id=1, source_target_pairs={{0,4},{4,8},{8,12},{1,5},{5,9},{9,13},{2,6},{6,10},{10,14},{3,7},{... | collective-permute-start | bytes 1179656 | tf_op jit(solution)/shard_map/ppermute | solution.py:24
  20.3 6.4 %collective-permute-done.3.refs_4_ = bf16[2,2,384,128]{3,2,1,0:T(8,128)(2,1)S(1)} collective-permute-done((bf16[2,2,384,128]{3,2,1,0:T(8,128)(2,1)}, bf16[2,2,384,128]{3,2,1,0:T(8,128)(2,1)S(1)}, u32[]{:S(2)}, u32[]{:S(2)}) %collective-permute-start.3) | collective-permute-done | bytes 393248 | tf_op jit(solution)/shard_map/ppermute | solution.py:24
  28.9 3.5 %collective-permute-start.6 = (bf16[2,2,384,128]{3,2,1,0:T(8,128)(2,1)S(1)}, bf16[2,2,384,128]{3,2,1,0:T(8,128)(2,1)S(1)}, u32[]{:S(2)}, u32[]{:S(2)}) collective-permute-start(bf16[2,2,384,128]{3,2,1,0:T(8,128)(2,1)S(1)} %collective-permute-done.5.refs_10_.refs_6_), channel_id=1, source_target_pairs={{0,4},{4,8},{8,12},{1,5},{5,9},{9,13},{2,6},{6,10},{10,14},{3,7},{... | collective-permute-start | bytes 1179656 | tf_op jit(solution)/shard_map/ppermute | solution.py:24
  36.3 2.8 %dynamic-slice_bitcast_fusion = (bf16[384,1536]{1,0:T(8,128)(2,1)S(1)}, bf16[384,1536]{1,0:T(8,128)(2,1)}) fusion(bf16[1,1,1,384,3072]{4,3,2,1,0:T(8,128)(2,1)} %param.8, s32[]{:T(128)S(6)} %select_n.7, s32[]{:T(128)S(6)} %select_n.6), kind=kLoop, calls=%fused_computation | loop fusion | bytes 4718600 | tf_op jit(solution)/shard_map/dynamic_slice | solution.py:487
  40.8 5.0 %collective-permute-done.12.refs_14_.refs_6_ = bf16[2,2,384,128]{3,2,1,0:T(8,128)(2,1)S(1)} collective-permute-done((bf16[2,2,384,128]{3,2,1,0:T(8,128)(2,1)S(1)}, bf16[2,2,384,128]{3,2,1,0:T(8,128)(2,1)S(1)}, u32[]{:S(2)}, u32[]{:S(2)}) %collective-permute-start.12) | collective-permute-done | bytes 393248 | tf_op jit(solution)/shard_map/ppermute | solution.py:24
  48.4 11.0 %shard_map.93 = (bf16[2,384,128]{2,1,0:T(8,128)(2,1)}, bf16[2,384,128]{2,1,0:T(8,128)(2,1)}, bf16[4,384,128]{2,1,0:T(8,128)(2,1)}, f32[4,384,128]{2,1,0:T(8,128)}, bf16[4,3,384,1152]{3,2,1,0:T(8,128)(2,1)}) custom-call(bf16[2,384,128]{2,1,0:T(8,128)(2,1)} %get-tuple-element.40.refs_0_, bf16[2,384,128]{2,1,0:T(8,128)(2,1)} %copy-done.3, ...), custom_call_target="tpu_custom_call" | custom-call | flops 2264924160 | bytes 17694720 | tf_op jit(solution)/shard_map/pallas_call | solution.py:51
  60.9 5.6 %collective-permute-done.15.refs_2_.refs_1_ = bf16[2,384,128]{2,1,0:T(8,128)(2,1)S(1)} collective-permute-done((bf16[2,384,128]{2,1,0:T(8,128)(2,1)}, bf16[2,384,128]{2,1,0:T(8,128)(2,1)S(1)}, u32[]{:S(2)}, u32[]{:S(2)}) %collective-permute-start.15) | collective-permute-done | bytes 196640 | tf_op jit(solution)/shard_map/ppermute | solution.py:18
  68.6 5.0 %shard_map.101 = (f32[256,768]{1,0:T(8,128)}, bf16[256,768]{1,0:T(8,128)(2,1)}, f32[256,768]{1,0:T(8,128)}, bf16[256,768]{1,0:T(8,128)(2,1)}) custom-call(bf16[2,384,128]{2,1,0:T(8,128)(2,1)} %get-tuple-element.44.refs_0_, bf16[2,384,128]{2,1,0:T(8,128)(2,1)} %copy-done.37, bf16[2,384,128]{2,1,0:T(8,128)(2,1)} %copy-done.38, ...), custom_call_target="tpu_custom_call" | custom-call | flops 1207959552 | bytes 5505024 | tf_op jit(solution)/shard_map/pallas_call | solution.py:51
  76.9 6.0 %shard_map.95 = (bf16[2,384,128]{2,1,0:T(8,128)(2,1)}, bf16[2,384,128]{2,1,0:T(8,128)(2,1)}) custom-call(bf16[384,3072]{1,0:T(8,128)(2,1)} %bitcast.12, bf16[256,3072]{1,0:T(8,128)(2,1)} %refs_1_.1, bf16[256,3072]{1,0:T(8,128)(2,1)} %copy-done, bf16[256,3072]{1,0:T(8,128)(2,1)} %copy-done.1), custom_call_target="tpu_custom_call" | custom-call | flops 1207959552 | bytes 7471104 | tf_op jit(solution)/shard_map/pallas_call | solution.py:51
  86.2 2.6 %shard_map.102 = (f32[128,768]{1,0:T(8,128)}, bf16[128,768]{1,0:T(8,128)(2,1)}, f32[128,768]{1,0:T(8,128)}, bf16[128,768]{1,0:T(8,128)(2,1)}) custom-call(f32[256,768]{1,0:T(8,128)} %get-tuple-element.63.refs_0_, bf16[256,768]{1,0:T(8,128)(2,1)} %copy-done.17, f32[256,768]{1,0:T(8,128)} %get-tuple-element.65.refs_2_, bf16[256,768]{1,0:T(8,128)(2,1)} %copy-done.18), custom_call_target="tpu_custom_call" | custom-call | bytes 3538944 | tf_op jit(solution)/shard_map/pallas_call | solution.py:51
  99.8 6.0 %collective-permute-start.36 = (bf16[32,1536]{1,0:T(8,128)(2,1)}, bf16[32,1536]{1,0:T(8,128)(2,1)S(1)}, u32[]{:S(2)}, u32[]{:S(2)}) collective-permute-start(bf16[32,1536]{1,0:T(8,128)(2,1)} %get-tuple-element.73), channel_id=1, source_target_pairs={{0,8},{4,12},{8,0},{12,4},{1,9},{5,13},{9,1},{13,5},{2,10},{6,14},... | collective-permute-start | bytes 294920 | tf_op jit(solution)/shard_map/ppermute | solution.py:18
  106.5 5.6 %shard_map.96 = (f32[4,384,128]{2,1,0:T(8,128)}, bf16[2,1536,128]{2,1,0:T(8,128)(2,1)}) custom-call(bf16[2,384,128]{2,1,0:T(8,128)(2,1)} %get-tuple-element.40.refs_0_, bf16[2,384,128]{2,1,0:T(8,128)(2,1)} %copy-done.3, bf16[2,384,128]{2,1,0:T(8,128)(2,1)} %copy-done.2, bf16[2,384,128]{2,1,0:T(8,128)(2,1)} %copy-done.4, bf16[2,2,384,128]{3,2,1,0:T(8,128)(2,1)} %copy-done.23, ...), custom_call_target="tpu_custom_call" | custom-call | flops 1509949440 | bytes 16515072 | tf_op jit(solution)/shard_map/pallas_call | solution.py:51
  112.2 8.0 %shard_map.97 = (f32[4,384,128]{2,1,0:T(8,128)}, bf16[2,1536,128]{2,1,0:T(8,128)(2,1)}) custom-call(bf16[2,384,128]{2,1,0:T(8,128)(2,1)} %get-tuple-element.40.refs_0_, bf16[2,384,128]{2,1,0:T(8,128)(2,1)} %copy-done.3, bf16[2,384,128]{2,1,0:T(8,128)(2,1)} %copy-done.2, bf16[2,384,128]{2,1,0:T(8,128)(2,1)} %copy-done.4, ...), custom_call_target="tpu_custom_call" | custom-call | flops 1509949440 | bytes 17301504 | tf_op jit(solution)/shard_map/pallas_call | solution.py:51
  120.2 6.0 %collective-permute-start.25 = (bf16[2,1536,128]{2,1,0:T(8,128)(2,1)}, bf16[2,1536,128]{2,1,0:T(8,128)(2,1)S(1)}, u32[]{:S(2)}, u32[]{:S(2)}) collective-permute-start(bf16[2,1536,128]{2,1,0:T(8,128)(2,1)} %get-tuple-element.56), channel_id=1, source_target_pairs={{0,4},{4,8},{8,12},{1,5},{5,9},{9,13},{2,6},{6,10},{10,14},{3,7},{... | collective-permute-start | bytes 2359304 | tf_op jit(solution)/shard_map/ppermute | solution.py:24
  127.7 2.7 %collective-permute-start.38 = (bf16[32,1536]{1,0:T(8,128)(2,1)S(1)}, bf16[32,1536]{1,0:T(8,128)(2,1)S(1)}, u32[]{:S(2)}, u32[]{:S(2)}) collective-permute-start(bf16[32,1536]{1,0:T(8,128)(2,1)S(1)} %add_convert_fusion.refs_0_), channel_id=1, source_target_pairs={{0,4},{4,0},{8,12},{12,8},{1,5},{5,1},{9,13},{13,9},{2,6},{6,2},{1... | collective-permute-start | bytes 294920 | tf_op jit(solution)/shard_map/ppermute | solution.py:18
  132.8 14.9 %collective-permute-done.38.refs_1_ = bf16[32,1536]{1,0:T(8,128)(2,1)S(1)} collective-permute-done((bf16[32,1536]{1,0:T(8,128)(2,1)S(1)}, bf16[32,1536]{1,0:T(8,128)(2,1)S(1)}, u32[]{:S(2)}, u32[]{:S(2)}) %collective-permute-start.38) | collective-permute-done | bytes 98336 | tf_op jit(solution)/shard_map/ppermute | solution.py:18
  147.7 2.9 %collective-permute-done.39.refs_2_ = bf16[32,1536]{1,0:T(8,128)(2,1)S(1)} collective-permute-done((bf16[32,1536]{1,0:T(8,128)(2,1)S(1)}, bf16[32,1536]{1,0:T(8,128)(2,1)S(1)}, u32[]{:S(2)}, u32[]{:S(2)}) %collective-permute-start.39) | collective-permute-done | bytes 98336 | tf_op jit(solution)/shard_map/ppermute | solution.py:18
  154.8 8.3 %shard_map.98 = (bf16[2,384,128]{2,1,0:T(8,128)(2,1)}, bf16[2,384,128]{2,1,0:T(8,128)(2,1)}, f32[2,1536,128]{2,1,0:T(8,128)}) custom-call(bf16[2,384,128]{2,1,0:T(8,128)(2,1)} %get-tuple-element.40.refs_0_, bf16[2,384,128]{2,1,0:T(8,128)(2,1)} %copy-done.3, bf16[2,384,128]{2,1,0:T(8,128)(2,1)} %copy-done.2, bf16[2,384,128]{2,1,0:T(8,128)(2,1)} %copy-done.4, ...), custom_call_target="tpu_custom_call" | custom-call | flops 1509949440 | bytes 17694720 | tf_op jit(solution)/shard_map/pallas_call | solution.py:51
  164.2 3.0 %shard_map.99 = (bf16[2,2,384,128]{3,2,1,0:T(8,128)(2,1)}, bf16[2,2,384,128]{3,2,1,0:T(8,128)(2,1)}) custom-call(f32[2,1536,128]{2,1,0:T(8,128)} %get-tuple-element.55.refs_0_, bf16[2,1536,128]{2,1,0:T(8,128)(2,1)} %copy-done.10, bf16[2,1536,128]{2,1,0:T(8,128)(2,1)} %copy-done.11), custom_call_target="tpu_custom_call" | custom-call | bytes 3932160 | tf_op jit(solution)/shard_map/pallas_call | solution.py:51
  169.7 7.5 %collective-permute-done.28.refs_6_ = bf16[2,2,384,128]{3,2,1,0:T(8,128)(2,1)S(1)} collective-permute-done((bf16[2,2,384,128]{3,2,1,0:T(8,128)(2,1)}, bf16[2,2,384,128]{3,2,1,0:T(8,128)(2,1)S(1)}, u32[]{:S(2)}, u32[]{:S(2)}) %collective-permute-start.28) | collective-permute-done | bytes 393248 | tf_op jit(solution)/shard_map/ppermute | solution.py:18
  181.8 5.5 %shard_map.94 = bf16[384,3072]{1,0:T(8,128)(2,1)} custom-call(bf16[2,384,128]{2,1,0:T(8,128)(2,1)} %get-tuple-element.44.refs_0_, bf16[2,384,128]{2,1,0:T(8,128)(2,1)} %copy-done.38, bf16[2,384,128]{2,1,0:T(8,128)(2,1)} %copy-done.37, bf16[2,384,128]{2,1,0:T(8,128)(2,1)} %copy-done.39, bf16[256,3072]{1,0:T(8,128)(2,1)} %refs_1_.1, ...), custom_call_target="tpu_custom_call" | custom-call | flops 1207959552 | bytes 7864320 | tf_op jit(solution)/shard_map/pallas_call | solution.py:51
  192.1 3.0 %shard_map.100 = (f32[384,512]{1,0:T(8,128)}, f32[384,512]{1,0:T(8,128)}, f32[384,512]{1,0:T(8,128)}) custom-call(bf16[2,384,128]{2,1,0:T(8,128)(2,1)} %get-tuple-element.53.refs_0_, bf16[2,384,128]{2,1,0:T(8,128)(2,1)} %copy-done.32, bf16[2,384,128]{2,1,0:T(8,128)(2,1)} %copy-done.31, bf16[2,384,128]{2,1,0:T(8,128)(2,1)} %copy-done.33, ...), custom_call_target="tpu_custom_call" | custom-call | bytes 4718592 | tf_op jit(solution)/shard_map/pallas_call | solution.py:51
  (171 shorter events, 59.8 us)
Async XLA Ops:
  0.6 33.3 %collective-permute-start.17 = (bf16[256,3072]{1,0:T(8,128)(2,1)}, bf16[256,3072]{1,0:T(8,128)(2,1)S(1)}, u32[]{:S(2)}, u32[]{:S(2)}) collective-permute-start(bf16[256,3072]{1,0:T(8,128)(2,1)} %refs_1_.1), channel_id=1, source_target_pairs={{0,16},{2,18},{16,0},{18,2},{4,20},{6,22},{20,4},{22,6},{8,24},{10... | collective-permute-start | bytes 4718600 | tf_op jit(solution)/shard_map/ppermute | solution.py:365
  13.8 12.8 %collective-permute-start.3 = (bf16[2,2,384,128]{3,2,1,0:T(8,128)(2,1)}, bf16[2,2,384,128]{3,2,1,0:T(8,128)(2,1)S(1)}, u32[]{:S(2)}, u32[]{:S(2)}) collective-permute-start(bf16[2,2,384,128]{3,2,1,0:T(8,128)(2,1)} %get-tuple-element.42.refs_8_.refs_4_), channel_id=1, source_target_pairs={{0,4},{4,8},{8,12},{1,5},{5,9},{9,13},{2,6},{6,10},{10,14},{3,7},{... | collective-permute-start | bytes 1179656 | tf_op jit(solution)/shard_map/ppermute | solution.py:24
  17.3 11.5 %collective-permute-start.5 = (bf16[2,2,384,128]{3,2,1,0:T(8,128)(2,1)}, bf16[2,2,384,128]{3,2,1,0:T(8,128)(2,1)S(1)}, u32[]{:S(2)}, u32[]{:S(2)}) collective-permute-start(bf16[2,2,384,128]{3,2,1,0:T(8,128)(2,1)} %get-tuple-element.43), channel_id=1, source_target_pairs={{0,2},{1,3},{2,0},{3,1},{4,6},{5,7},{6,4},{7,5},{8,10},{9,11},{10,... | collective-permute-start | bytes 1179656 | tf_op jit(solution)/shard_map/ppermute | solution.py:18
  18.9 13.4 %collective-permute-start.8 = (bf16[2,2,384,128]{3,2,1,0:T(8,128)(2,1)}, bf16[2,2,384,128]{3,2,1,0:T(8,128)(2,1)S(1)}, u32[]{:S(2)}, u32[]{:S(2)}) collective-permute-start(bf16[2,2,384,128]{3,2,1,0:T(8,128)(2,1)} %get-tuple-element.42.refs_8_.refs_4_), channel_id=1, source_target_pairs={{0,1},{1,0},{2,3},{3,2},{4,5},{5,4},{6,7},{7,6},{8,9},{9,8},{10,11... | collective-permute-start | bytes 1179656 | tf_op jit(solution)/shard_map/ppermute | solution.py:18
  19.0 13.7 %collective-permute-start.10 = (bf16[2,2,384,128]{3,2,1,0:T(8,128)(2,1)}, bf16[2,2,384,128]{3,2,1,0:T(8,128)(2,1)}, u32[]{:S(2)}, u32[]{:S(2)}) collective-permute-start(bf16[2,2,384,128]{3,2,1,0:T(8,128)(2,1)} %get-tuple-element.42.refs_8_.refs_4_), channel_id=1, source_target_pairs={{4,0},{8,4},{12,8},{5,1},{9,5},{13,9},{6,2},{10,6},{14,10},{7,3},{... | collective-permute-start | bytes 1179656 | tf_op jit(solution)/shard_map/ppermute | solution.py:24
  26.7 12.5 %collective-permute-start.4 = (bf16[2,2,384,128]{3,2,1,0:T(8,128)(2,1)S(1)}, bf16[2,2,384,128]{3,2,1,0:T(8,128)(2,1)}, u32[]{:S(2)}, u32[]{:S(2)}) collective-permute-start(bf16[2,2,384,128]{3,2,1,0:T(8,128)(2,1)S(1)} %collective-permute-done.3.refs_4_), channel_id=1, source_target_pairs={{0,1},{1,0},{2,3},{3,2},{4,5},{5,4},{6,7},{7,6},{8,9},{9,8},{10,11... | collective-permute-start | bytes 1179656 | tf_op jit(solution)/shard_map/ppermute | solution.py:18
  32.7 13.2 %collective-permute-start.12 = (bf16[2,2,384,128]{3,2,1,0:T(8,128)(2,1)S(1)}, bf16[2,2,384,128]{3,2,1,0:T(8,128)(2,1)S(1)}, u32[]{:S(2)}, u32[]{:S(2)}) collective-permute-start(bf16[2,2,384,128]{3,2,1,0:T(8,128)(2,1)S(1)} %collective-permute-done.5.refs_10_.refs_6_), channel_id=1, source_target_pairs={{4,0},{8,4},{12,8},{5,1},{9,5},{13,9},{6,2},{10,6},{14,10},{7,3},{... | collective-permute-start | bytes 1179656 | tf_op jit(solution)/shard_map/ppermute | solution.py:24
  34.0 41.7 %collective-permute-start.18 = (bf16[256,3072]{1,0:T(8,128)(2,1)S(1)}, bf16[256,3072]{1,0:T(8,128)(2,1)S(1)}, u32[]{:S(2)}, u32[]{:S(2)}) collective-permute-start(bf16[256,3072]{1,0:T(8,128)(2,1)S(1)} %collective-permute-done.17.refs_5_.refs_2_), channel_id=1, source_target_pairs={{0,1},{2,3},{4,5},{6,7},{8,9},{10,11},{12,13},{14,15},{16,17},{18,... | collective-permute-start | bytes 4718600 | tf_op jit(solution)/shard_map/ppermute | solution.py:366
  39.1 27.4 %collective-permute-start.30 = (bf16[384,1536]{1,0:T(8,128)(2,1)S(1)}, bf16[384,1536]{1,0:T(8,128)(2,1)}, u32[]{:S(2)}, u32[]{:S(2)}) collective-permute-start(bf16[384,1536]{1,0:T(8,128)(2,1)S(1)} %get-tuple-element.75), channel_id=1, source_target_pairs={{0,1},{1,0},{2,3},{3,2},{4,5},{5,4},{6,7},{7,6},{8,9},{9,8},{10,11... | collective-permute-start | bytes 3538952 | tf_op jit(solution)/shard_map/ppermute | solution.py:18
  92.7 13.1 %collective-permute-start.19 = (bf16[2,384,128]{2,1,0:T(8,128)(2,1)S(1)}, bf16[2,384,128]{2,1,0:T(8,128)(2,1)S(1)}, u32[]{:S(2)}, u32[]{:S(2)}) collective-permute-start(bf16[2,384,128]{2,1,0:T(8,128)(2,1)S(1)} %copy-done.5), channel_id=1, source_target_pairs={{0,1},{1,0},{2,3},{3,2},{4,5},{5,4},{6,7},{7,6},{8,9},{9,8},{10,11... | collective-permute-start | bytes 589832 | tf_op jit(solution)/shard_map/ppermute | solution.py:18
  92.7 13.1 %collective-permute-start.21 = (bf16[2,384,128]{2,1,0:T(8,128)(2,1)S(1)}, bf16[2,384,128]{2,1,0:T(8,128)(2,1)S(1)}, u32[]{:S(2)}, u32[]{:S(2)}) collective-permute-start(bf16[2,384,128]{2,1,0:T(8,128)(2,1)S(1)} %collective-permute-done.20.refs_10_), channel_id=1, source_target_pairs={{0,1},{1,0},{2,3},{3,2},{4,5},{5,4},{6,7},{7,6},{8,9},{9,8},{10,11... | collective-permute-start | bytes 589832 | tf_op jit(solution)/shard_map/ppermute | solution.py:18
  99.8 27.8 %collective-permute-start.37 = (bf16[32,1536]{1,0:T(8,128)(2,1)}, bf16[32,1536]{1,0:T(8,128)(2,1)S(1)}, u32[]{:S(2)}, u32[]{:S(2)}) collective-permute-start(bf16[32,1536]{1,0:T(8,128)(2,1)} %get-tuple-element.74), channel_id=1, source_target_pairs={{0,12},{4,8},{8,4},{12,0},{1,13},{5,9},{9,5},{13,1},{2,14},{6,10},... | collective-permute-start | bytes 294920 | tf_op jit(solution)/shard_map/ppermute | solution.py:18
  99.8 27.8 %collective-permute-start.36 = (bf16[32,1536]{1,0:T(8,128)(2,1)}, bf16[32,1536]{1,0:T(8,128)(2,1)S(1)}, u32[]{:S(2)}, u32[]{:S(2)}) collective-permute-start(bf16[32,1536]{1,0:T(8,128)(2,1)} %get-tuple-element.73), channel_id=1, source_target_pairs={{0,8},{4,12},{8,0},{12,4},{1,9},{5,13},{9,1},{13,5},{2,10},{6,14},... | collective-permute-start | bytes 294920 | tf_op jit(solution)/shard_map/ppermute | solution.py:18
  105.8 21.8 %collective-permute-start.35 = (bf16[32,1536]{1,0:T(8,128)(2,1)}, bf16[32,1536]{1,0:T(8,128)(2,1)S(1)}, u32[]{:S(2)}, u32[]{:S(2)}) collective-permute-start(bf16[32,1536]{1,0:T(8,128)(2,1)} %get-tuple-element.72), channel_id=1, source_target_pairs={{0,4},{4,0},{8,12},{12,8},{1,5},{5,1},{9,13},{13,9},{2,6},{6,2},{1... | collective-permute-start | bytes 294920 | tf_op jit(solution)/shard_map/ppermute | solution.py:18
  120.2 42.9 %collective-permute-start.25 = (bf16[2,1536,128]{2,1,0:T(8,128)(2,1)}, bf16[2,1536,128]{2,1,0:T(8,128)(2,1)S(1)}, u32[]{:S(2)}, u32[]{:S(2)}) collective-permute-start(bf16[2,1536,128]{2,1,0:T(8,128)(2,1)} %get-tuple-element.56), channel_id=1, source_target_pairs={{0,4},{4,8},{8,12},{1,5},{5,9},{9,13},{2,6},{6,10},{10,14},{3,7},{... | collective-permute-start | bytes 2359304 | tf_op jit(solution)/shard_map/ppermute | solution.py:24
  126.2 36.9 %collective-permute-start.26 = (bf16[2,1536,128]{2,1,0:T(8,128)(2,1)S(1)}, bf16[2,1536,128]{2,1,0:T(8,128)(2,1)S(1)}, u32[]{:S(2)}, u32[]{:S(2)}) collective-permute-start(bf16[2,1536,128]{2,1,0:T(8,128)(2,1)S(1)} %copy-done.43), channel_id=1, source_target_pairs={{4,0},{8,4},{12,8},{5,1},{9,5},{13,9},{6,2},{10,6},{14,10},{7,3},{... | collective-permute-start | bytes 2359304 | tf_op jit(solution)/shard_map/ppermute | solution.py:24
  127.7 20.0 %collective-permute-start.38 = (bf16[32,1536]{1,0:T(8,128)(2,1)S(1)}, bf16[32,1536]{1,0:T(8,128)(2,1)S(1)}, u32[]{:S(2)}, u32[]{:S(2)}) collective-permute-start(bf16[32,1536]{1,0:T(8,128)(2,1)S(1)} %add_convert_fusion.refs_0_), channel_id=1, source_target_pairs={{0,4},{4,0},{8,12},{12,8},{1,5},{5,1},{9,13},{13,9},{2,6},{6,2},{1... | collective-permute-start | bytes 294920 | tf_op jit(solution)/shard_map/ppermute | solution.py:18
  130.4 20.2 %collective-permute-start.39 = (bf16[32,1536]{1,0:T(8,128)(2,1)S(1)}, bf16[32,1536]{1,0:T(8,128)(2,1)S(1)}, u32[]{:S(2)}, u32[]{:S(2)}) collective-permute-start(bf16[32,1536]{1,0:T(8,128)(2,1)S(1)} %add_convert_fusion.refs_0_), channel_id=1, source_target_pairs={{0,8},{4,12},{8,0},{12,4},{1,9},{5,13},{9,1},{13,5},{2,10},{6,14},... | collective-permute-start | bytes 294920 | tf_op jit(solution)/shard_map/ppermute | solution.py:18
  130.4 20.2 %collective-permute-start.40 = (bf16[32,1536]{1,0:T(8,128)(2,1)S(1)}, bf16[32,1536]{1,0:T(8,128)(2,1)S(1)}, u32[]{:S(2)}, u32[]{:S(2)}) collective-permute-start(bf16[32,1536]{1,0:T(8,128)(2,1)S(1)} %add_convert_fusion.refs_0_), channel_id=1, source_target_pairs={{0,12},{4,8},{8,4},{12,0},{1,13},{5,9},{9,5},{13,1},{2,14},{6,10},... | collective-permute-start | bytes 294920 | tf_op jit(solution)/shard_map/ppermute | solution.py:18
  153.6 14.4 %collective-permute-start.42 = (bf16[128,1536]{1,0:T(8,128)(2,1)}, bf16[128,1536]{1,0:T(8,128)(2,1)S(1)}, u32[]{:S(2)}, u32[]{:S(2)}) collective-permute-start(bf16[128,1536]{1,0:T(8,128)(2,1)} %shard_map.104.refs_0_), channel_id=1, source_target_pairs={{0,2},{1,3},{2,0},{3,1},{4,6},{5,7},{6,4},{7,5},{8,10},{9,11},{10,... | collective-permute-start | bytes 1179656 | tf_op jit(solution)/shard_map/ppermute | solution.py:18
  168.1 19.2 %collective-permute-start.43 = (bf16[128,1536]{1,0:T(8,128)(2,1)S(1)}, bf16[128,1536]{1,0:T(8,128)(2,1)S(1)}, u32[]{:S(2)}, u32[]{:S(2)}) collective-permute-start(bf16[128,1536]{1,0:T(8,128)(2,1)S(1)} %collective-permute-done.42.refs_1_), channel_id=1, source_target_pairs={{0,1},{1,0},{2,3},{3,2},{4,5},{5,4},{6,7},{7,6},{8,9},{9,8},{10,11... | collective-permute-start | bytes 1179656 | tf_op jit(solution)/shard_map/ppermute | solution.py:18
  169.7 20.7 %collective-permute-start.27 = (bf16[2,2,384,128]{3,2,1,0:T(8,128)(2,1)}, bf16[2,2,384,128]{3,2,1,0:T(8,128)(2,1)S(1)}, u32[]{:S(2)}, u32[]{:S(2)}) collective-permute-start(bf16[2,2,384,128]{3,2,1,0:T(8,128)(2,1)} %get-tuple-element.58.refs_4_), channel_id=1, source_target_pairs={{0,1},{1,0},{2,3},{3,2},{4,5},{5,4},{6,7},{7,6},{8,9},{9,8},{10,11... | collective-permute-start | bytes 1179656 | tf_op jit(solution)/shard_map/ppermute | solution.py:18
  177.3 13.1 %collective-permute-start.29 = (bf16[2,2,384,128]{3,2,1,0:T(8,128)(2,1)S(1)}, bf16[2,2,384,128]{3,2,1,0:T(8,128)(2,1)S(1)}, u32[]{:S(2)}, u32[]{:S(2)}) collective-permute-start(bf16[2,2,384,128]{3,2,1,0:T(8,128)(2,1)S(1)} %collective-permute-done.28.refs_6_), channel_id=1, source_target_pairs={{0,1},{1,0},{2,3},{3,2},{4,5},{5,4},{6,7},{7,6},{8,9},{9,8},{10,11... | collective-permute-start | bytes 1179656 | tf_op jit(solution)/shard_map/ppermute | solution.py:18
  177.3 13.1 %collective-permute-start.22 = (bf16[2,384,128]{2,1,0:T(8,128)(2,1)S(1)}, bf16[2,384,128]{2,1,0:T(8,128)(2,1)S(1)}, u32[]{:S(2)}, u32[]{:S(2)}) collective-permute-start(bf16[2,384,128]{2,1,0:T(8,128)(2,1)S(1)} %copy-done.30), channel_id=1, source_target_pairs={{0,1},{1,0},{2,3},{3,2},{4,5},{5,4},{6,7},{7,6},{8,9},{9,8},{10,11... | collective-permute-start | bytes 589832 | tf_op jit(solution)/shard_map/ppermute | solution.py:18
  (65 other events, 412.5 us)

commit v2 on v1

--- a/solution.py
+++ b/solution.py
@@ -323,20 +323,17 @@
         target[:, wide:] = right.astype(target.dtype)
 
 
-def place_rows_kernel(sc, *refs):
-    size = refs[0].shape[0]
-    for m in range(len(refs) - 1):
-        refs[-1][pl.ds(pl.multiple_of((sc[9] ^ m) * size, size), size), :] = refs[m][...]
-
-
 def place_final_kernel(sc, *refs):
-    @pl.when(pl.program_id(0) == sc[10])
-    def _():
-        refs[-1][...] = refs[-3][...].astype(F32)
-
-    @pl.when(pl.program_id(0) != sc[10])
-    def _():
-        refs[-1][...] = refs[-2][...].astype(F32)
+    out = refs[-1]
+    size = refs[-2].shape[0]
+    column = pl.program_id(0)
+    for mine, pieces in ((True, refs[-9:-5]), (False, refs[-5:-1])):
+
+        @pl.when((column == sc[10]) if mine else (column != sc[10]))
+        def _():
+            for m in range(4):
+                at = pl.ds(pl.multiple_of((sc[9] ^ m) * size, size), size)
+                out[at, :] = pieces[m][...].astype(F32)
 
 
 def on_device(query_in, key_in, value_in, grad_out, out_weight):
@@ -521,25 +518,26 @@
         got = [xor_send(sends[m - 1], "ha", m) for m in (1, 2, 3)]
         piece = (keep + got[0].astype(F32) + got[1].astype(F32) + got[2].astype(F32)).astype(BF)
         pieces = [piece] + [xor_send(piece, "ha", m) for m in (1, 2, 3)]
-        (piece,) = call(place_rows_kernel, pieces, [sds((4 * rows, half), BF)])
-        other = across(piece)
+        others = [across(value) for value in pieces]
+        near_pieces = pieces + [partner(value) for value in pieces]
+        far_pieces = others + [partner(value) for value in others]
 
         def rows_of(flip):
             return pl.BlockSpec((share // 2, half), lambda j: ((lax.axis_index("wa") >> 1) ^ flip, j))
 
         (begun,) = call(
             place_final_kernel,
-            [piece, partner(piece)],
+            near_pieces,
             [sds((share, model), F32)],
             grid=(2,),
             out_specs=[rows_of(0)],
         )
         (weight_grad,) = call(
             place_final_kernel,
-            [begun, other, partner(other)],
+            [begun] + far_pieces,
             [sds((share, model), F32)],
             grid=(2,),
-            in_specs=[pl.BlockSpec(memory_space=pl.ANY), None, None],
+            in_specs=[pl.BlockSpec(memory_space=pl.ANY)] + [None] * 8,
             out_specs=[rows_of(1)],
             alias={0: 0},
         )

time: 196 us -> 203 us (1.036)
  waiting for transfers between devices: 60.8 us -> 69.6 us
    ppermute x1, waiting for transfers between devices: 0.01 us -> 18.6 us  [on_device(): w_even = lax.ppermute(out_weight, ('dp', 'wa'), swap)]
    ppermute x6, waiting for transfers between devices: 12.8 us -> 7.63 us  [step_send(): return lax.ppermute(value, axis, pairs)]
    ppermute x36 -> x45, waiting for transfers between devices: 48 us -> 43.4 us  [xor_send(): return lax.ppermute(value, axis, [(i, i ^ mask) for i in range(count)])]
    ppermute x6, starting transfers between devices: 16.8 us -> 20.8 us  [step_send(): return lax.ppermute(value, axis, pairs)]
    ppermute x36 -> x45, starting transfers between devices: 27.6 us -> 25.1 us  [xor_send(): return lax.ppermute(value, axis, [(i, i ^ mask) for i in range(count)])]
    pallas_call x15 -> x14, Pallas kernels: 69.1 us -> 67.4 us  [call(): pl.pallas_call(lambda *refs: kernel(place_of(), *refs), out_shape=list(ou...]
    unnamed x90 -> x102, local copies, waits for them, and re-layouts: 9.58 us -> 9.32 us
  transfers between devices with their start and end apart: 44 -> 53, of which waited for: 17 -> 19; matrix products, arithmetic and copies ran while one was open for 1% -> 1% of each run, Pallas kernels for 34% -> 32%
where the time goes in v2:
time: 203 us
  waiting for transfers between devices  69.6 us (34%)
  Pallas kernels  67.4 us (33%)
  starting transfers between devices  52.1 us (26%)
  local copies, waits for them, and re-layouts  12.1 us (6%)
    pallas_call x14, Pallas kernels, call(): pl.pallas_call(lambda *refs: kernel(place_of(), *refs), out_shape=list(ou...  67.4 us
    ppermute x45, waiting for transfers between devices, xor_send(): return lax.ppermute(value, axis, [(i, i ^ mask) for i in range(count)])  43.4 us
    ppermute x45, starting transfers between devices, xor_send(): return lax.ppermute(value, axis, [(i, i ^ mask) for i in range(count)])  25.1 us
    ppermute x6, starting transfers between devices, step_send(): return lax.ppermute(value, axis, pairs)  20.8 us
    ppermute x1, waiting for transfers between devices, on_device(): w_even = lax.ppermute(out_weight, ('dp', 'wa'), swap)  18.6 us
    unnamed x102, local copies, waits for them, and re-layouts  9.32 us
    ppermute x6, waiting for transfers between devices, step_send(): return lax.ppermute(value, axis, pairs)  7.63 us
    ppermute x1, starting transfers between devices, on_device(): w_even = lax.ppermute(out_weight, ('dp', 'wa'), swap)  4.88 us
  transfers between devices with their start and end apart: 53, of which 19 were waited for; matrix products, arithmetic and copies ran while one was open for 1% of the time, Pallas kernels for 32%

profile of v2, /device:TPU:0, one launch (start us, length us, event | category | flops | bytes accessed | tf_op | source)
XLA Modules:
  0.0 202.6 jit_solution(15496245851572611606)
XLA Ops:
  0.6 4.9 %collective-permute-start.17 = (bf16[256,3072]{1,0:T(8,128)(2,1)}, bf16[256,3072]{1,0:T(8,128)(2,1)S(1)}, u32[]{:S(2)}, u32[]{:S(2)}) collective-permute-start(bf16[256,3072]{1,0:T(8,128)(2,1)} %refs_1_.1), channel_id=1, source_target_pairs={{0,16},{2,18},{16,0},{18,2},{4,20},{6,22},{20,4},{22,6},{8,24},{10... | collective-permute-start | bytes 4718600 | tf_op jit(solution)/shard_map/ppermute | solution.py:362
  5.5 18.6 %collective-permute-done.17.refs_5_.refs_2_ = bf16[256,3072]{1,0:T(8,128)(2,1)S(1)} collective-permute-done((bf16[256,3072]{1,0:T(8,128)(2,1)}, bf16[256,3072]{1,0:T(8,128)(2,1)S(1)}, u32[]{:S(2)}, u32[]{:S(2)}) %collective-permute-start.17) | collective-permute-done | bytes 1572896 | tf_op jit(solution)/shard_map/ppermute | solution.py:362
  30.1 4.7 %collective-permute-start.3 = (bf16[2,2,384,128]{3,2,1,0:T(8,128)(2,1)}, bf16[2,2,384,128]{3,2,1,0:T(8,128)(2,1)}, u32[]{:S(2)}, u32[]{:S(2)}) collective-permute-start(bf16[2,2,384,128]{3,2,1,0:T(8,128)(2,1)} %get-tuple-element.42.refs_8_.refs_4_), channel_id=1, source_target_pairs={{0,4},{4,8},{8,12},{1,5},{5,9},{9,13},{2,6},{6,10},{10,14},{3,7},{... | collective-permute-start | bytes 1179656 | tf_op jit(solution)/shard_map/ppermute | solution.py:24
  39.4 4.9 %collective-permute-done.5.refs_10_.refs_6_ = bf16[2,2,384,128]{3,2,1,0:T(8,128)(2,1)} collective-permute-done((bf16[2,2,384,128]{3,2,1,0:T(8,128)(2,1)}, bf16[2,2,384,128]{3,2,1,0:T(8,128)(2,1)}, u32[]{:S(2)}, u32[]{:S(2)}) %collective-permute-start.5) | collective-permute-done | bytes 393248 | tf_op jit(solution)/shard_map/ppermute | solution.py:18
  44.3 3.7 %collective-permute-start.6 = (bf16[2,2,384,128]{3,2,1,0:T(8,128)(2,1)}, bf16[2,2,384,128]{3,2,1,0:T(8,128)(2,1)S(1)}, u32[]{:S(2)}, u32[]{:S(2)}) collective-permute-start(bf16[2,2,384,128]{3,2,1,0:T(8,128)(2,1)} %collective-permute-done.5.refs_10_.refs_6_), channel_id=1, source_target_pairs={{0,4},{4,8},{8,12},{1,5},{5,9},{9,13},{2,6},{6,10},{10,14},{3,7},{... | collective-permute-start | bytes 1179656 | tf_op jit(solution)/shard_map/ppermute | solution.py:24
  49.4 2.8 %dynamic-slice_bitcast_fusion = (bf16[384,1536]{1,0:T(8,128)(2,1)S(1)}, bf16[384,1536]{1,0:T(8,128)(2,1)}) fusion(bf16[1,1,1,384,3072]{4,3,2,1,0:T(8,128)(2,1)} %param.8, s32[]{:T(128)S(6)} %select_n.7, s32[]{:T(128)S(6)} %select_n.6), kind=kLoop, calls=%fused_computation | loop fusion | bytes 4718600 | tf_op jit(solution)/shard_map/dynamic_slice | solution.py:484
  52.9 3.6 %collective-permute-done.6.refs_6_ = bf16[2,2,384,128]{3,2,1,0:T(8,128)(2,1)S(1)} collective-permute-done((bf16[2,2,384,128]{3,2,1,0:T(8,128)(2,1)}, bf16[2,2,384,128]{3,2,1,0:T(8,128)(2,1)S(1)}, u32[]{:S(2)}, u32[]{:S(2)}) %collective-permute-start.6) | collective-permute-done | bytes 393248 | tf_op jit(solution)/shard_map/ppermute | solution.py:24
  56.5 4.0 %collective-permute-done.12.refs_14_.refs_6_ = bf16[2,2,384,128]{3,2,1,0:T(8,128)(2,1)S(1)} collective-permute-done((bf16[2,2,384,128]{3,2,1,0:T(8,128)(2,1)}, bf16[2,2,384,128]{3,2,1,0:T(8,128)(2,1)S(1)}, u32[]{:S(2)}, u32[]{:S(2)}) %collective-permute-start.12) | collective-permute-done | bytes 393248 | tf_op jit(solution)/shard_map/ppermute | solution.py:24
  61.7 6.0 %shard_map.95 = (bf16[2,384,128]{2,1,0:T(8,128)(2,1)}, bf16[2,384,128]{2,1,0:T(8,128)(2,1)}) custom-call(bf16[384,3072]{1,0:T(8,128)(2,1)} %bitcast.12, bf16[256,3072]{1,0:T(8,128)(2,1)} %refs_1_.1, bf16[256,3072]{1,0:T(8,128)(2,1)} %copy-done, bf16[256,3072]{1,0:T(8,128)(2,1)} %copy-done.1), custom_call_target="tpu_custom_call" | custom-call | flops 1207959552 | bytes 7471104 | tf_op jit(solution)/shard_map/pallas_call | solution.py:51
  71.0 11.0 %shard_map.93 = (bf16[2,384,128]{2,1,0:T(8,128)(2,1)}, bf16[2,384,128]{2,1,0:T(8,128)(2,1)}, bf16[4,384,128]{2,1,0:T(8,128)(2,1)}, f32[4,384,128]{2,1,0:T(8,128)}, bf16[4,3,384,1152]{3,2,1,0:T(8,128)(2,1)}) custom-call(bf16[2,384,128]{2,1,0:T(8,128)(2,1)} %get-tuple-element.40.refs_0_, bf16[2,384,128]{2,1,0:T(8,128)(2,1)} %copy-done.2, ...), custom_call_target="tpu_custom_call" | custom-call | flops 2264924160 | bytes 17694720 | tf_op jit(solution)/shard_map/pallas_call | solution.py:51
  83.1 6.1 %collective-permute-done.15.refs_2_.refs_1_ = bf16[2,384,128]{2,1,0:T(8,128)(2,1)S(1)} collective-permute-done((bf16[2,384,128]{2,1,0:T(8,128)(2,1)}, bf16[2,384,128]{2,1,0:T(8,128)(2,1)S(1)}, u32[]{:S(2)}, u32[]{:S(2)}) %collective-permute-start.15) | collective-permute-done | bytes 196640 | tf_op jit(solution)/shard_map/ppermute | solution.py:18
  90.0 5.6 %shard_map.96 = (f32[4,384,128]{2,1,0:T(8,128)}, bf16[2,1536,128]{2,1,0:T(8,128)(2,1)}) custom-call(bf16[2,384,128]{2,1,0:T(8,128)(2,1)} %get-tuple-element.40.refs_0_, bf16[2,384,128]{2,1,0:T(8,128)(2,1)} %copy-done.2, bf16[2,384,128]{2,1,0:T(8,128)(2,1)} %copy-done.3, bf16[2,384,128]{2,1,0:T(8,128)(2,1)} %copy-done.4, ...), custom_call_target="tpu_custom_call" | custom-call | flops 1509949440 | bytes 16515072 | tf_op jit(solution)/shard_map/pallas_call | solution.py:51
  95.6 8.0 %shard_map.97 = (f32[4,384,128]{2,1,0:T(8,128)}, bf16[2,1536,128]{2,1,0:T(8,128)(2,1)}) custom-call(bf16[2,384,128]{2,1,0:T(8,128)(2,1)} %get-tuple-element.40.refs_0_, bf16[2,384,128]{2,1,0:T(8,128)(2,1)} %copy-done.2, bf16[2,384,128]{2,1,0:T(8,128)(2,1)} %copy-done.3, bf16[2,384,128]{2,1,0:T(8,128)(2,1)} %copy-done.4, ...), custom_call_target="tpu_custom_call" | custom-call | flops 1509949440 | bytes 17301504 | tf_op jit(solution)/shard_map/pallas_call | solution.py:51
  103.6 8.5 %collective-permute-start.25 = (bf16[2,1536,128]{2,1,0:T(8,128)(2,1)}, bf16[2,1536,128]{2,1,0:T(8,128)(2,1)S(1)}, u32[]{:S(2)}, u32[]{:S(2)}) collective-permute-start(bf16[2,1536,128]{2,1,0:T(8,128)(2,1)} %get-tuple-element.56), channel_id=1, source_target_pairs={{0,4},{4,8},{8,12},{1,5},{5,9},{9,13},{2,6},{6,10},{10,14},{3,7},{... | collective-permute-start | bytes 2359304 | tf_op jit(solution)/shard_map/ppermute | solution.py:24
  114.2 5.0 %shard_map.101 = (f32[256,768]{1,0:T(8,128)}, bf16[256,768]{1,0:T(8,128)(2,1)}, f32[256,768]{1,0:T(8,128)}, bf16[256,768]{1,0:T(8,128)(2,1)}) custom-call(bf16[2,384,128]{2,1,0:T(8,128)(2,1)} %get-tuple-element.44.refs_0_, bf16[2,384,128]{2,1,0:T(8,128)(2,1)} %copy-done.31, bf16[2,384,128]{2,1,0:T(8,128)(2,1)} %copy-done.32, ...), custom_call_target="tpu_custom_call" | custom-call | flops 1207959552 | bytes 5505024 | tf_op jit(solution)/shard_map/pallas_call | solution.py:51
  121.2 9.4 %collective-permute-done.31.refs_1_ = bf16[256,768]{1,0:T(8,128)(2,1)S(1)} collective-permute-done((bf16[256,768]{1,0:T(8,128)(2,1)}, bf16[256,768]{1,0:T(8,128)(2,1)S(1)}, u32[]{:S(2)}, u32[]{:S(2)}) %collective-permute-start.31) | collective-permute-done | bytes 393248 | tf_op jit(solution)/shard_map/ppermute | solution.py:18
  132.6 2.6 %shard_map.102 = (f32[128,768]{1,0:T(8,128)}, bf16[128,768]{1,0:T(8,128)(2,1)}, f32[128,768]{1,0:T(8,128)}, bf16[128,768]{1,0:T(8,128)(2,1)}) custom-call(f32[256,768]{1,0:T(8,128)} %get-tuple-element.63.refs_0_, bf16[256,768]{1,0:T(8,128)(2,1)} %copy-done.14, f32[256,768]{1,0:T(8,128)} %get-tuple-element.65.refs_2_, bf16[256,768]{1,0:T(8,128)(2,1)} %copy-done.15), custom_call_target="tpu_custom_call" | custom-call | bytes 3538944 | tf_op jit(solution)/shard_map/pallas_call | solution.py:51
  136.3 5.0 %collective-permute-done.33.refs_1_ = bf16[128,768]{1,0:T(8,128)(2,1)S(1)} collective-permute-done((bf16[128,768]{1,0:T(8,128)(2,1)}, bf16[128,768]{1,0:T(8,128)(2,1)S(1)}, u32[]{:S(2)}, u32[]{:S(2)}) %collective-permute-start.33) | collective-permute-done | bytes 196640 | tf_op jit(solution)/shard_map/ppermute | solution.py:18
  144.4 3.1 %collective-permute-start.37 = (bf16[32,1536]{1,0:T(8,128)(2,1)}, bf16[32,1536]{1,0:T(8,128)(2,1)S(1)}, u32[]{:S(2)}, u32[]{:S(2)}) collective-permute-start(bf16[32,1536]{1,0:T(8,128)(2,1)} %get-tuple-element.74), channel_id=1, source_target_pairs={{0,12},{4,8},{8,4},{12,0},{1,13},{5,9},{9,5},{13,1},{2,14},{6,10},... | collective-permute-start | bytes 294920 | tf_op jit(solution)/shard_map/ppermute | solution.py:18
  148.8 8.3 %shard_map.98 = (bf16[2,384,128]{2,1,0:T(8,128)(2,1)}, bf16[2,384,128]{2,1,0:T(8,128)(2,1)}, f32[2,1536,128]{2,1,0:T(8,128)}) custom-call(bf16[2,384,128]{2,1,0:T(8,128)(2,1)} %get-tuple-element.40.refs_0_, bf16[2,384,128]{2,1,0:T(8,128)(2,1)} %copy-done.2, bf16[2,384,128]{2,1,0:T(8,128)(2,1)} %copy-done.3, bf16[2,384,128]{2,1,0:T(8,128)(2,1)} %copy-done.4, ...), custom_call_target="tpu_custom_call" | custom-call | flops 1509949440 | bytes 17694720 | tf_op jit(solution)/shard_map/pallas_call | solution.py:51
  158.2 2.9 %shard_map.99 = (bf16[2,2,384,128]{3,2,1,0:T(8,128)(2,1)}, bf16[2,2,384,128]{3,2,1,0:T(8,128)(2,1)}) custom-call(f32[2,1536,128]{2,1,0:T(8,128)} %get-tuple-element.55.refs_0_, bf16[2,1536,128]{2,1,0:T(8,128)(2,1)} %copy-done.9, bf16[2,1536,128]{2,1,0:T(8,128)(2,1)} %copy-done.10), custom_call_target="tpu_custom_call" | custom-call | bytes 3932160 | tf_op jit(solution)/shard_map/pallas_call | solution.py:51
  176.1 3.1 %collective-permute-done.46.refs_2_ = bf16[32,1536]{1,0:T(8,128)(2,1)S(1)} collective-permute-done((bf16[32,1536]{1,0:T(8,128)(2,1)S(1)}, bf16[32,1536]{1,0:T(8,128)(2,1)S(1)}, u32[]{:S(2)}, u32[]{:S(2)}) %collective-permute-start.46) | collective-permute-done | bytes 98336 | tf_op jit(solution)/shard_map/ppermute | solution.py:18
  192.4 5.5 %shard_map.94 = bf16[384,3072]{1,0:T(8,128)(2,1)} custom-call(bf16[2,384,128]{2,1,0:T(8,128)(2,1)} %get-tuple-element.44.refs_0_, bf16[2,384,128]{2,1,0:T(8,128)(2,1)} %copy-done.32, bf16[2,384,128]{2,1,0:T(8,128)(2,1)} %copy-done.31, bf16[2,384,128]{2,1,0:T(8,128)(2,1)} %copy-done.33, bf16[256,3072]{1,0:T(8,128)(2,1)} %refs_1_.1, ...), custom_call_target="tpu_custom_call" | custom-call | flops 1207959552 | bytes 7864320 | tf_op jit(solution)/shard_map/pallas_call | solution.py:51
  199.6 3.0 %shard_map.100 = (f32[384,512]{1,0:T(8,128)}, f32[384,512]{1,0:T(8,128)}, f32[384,512]{1,0:T(8,128)}) custom-call(bf16[2,384,128]{2,1,0:T(8,128)(2,1)} %get-tuple-element.53.refs_0_, bf16[2,384,128]{2,1,0:T(8,128)(2,1)} %copy-done.26, bf16[2,384,128]{2,1,0:T(8,128)(2,1)} %copy-done.25, bf16[2,384,128]{2,1,0:T(8,128)(2,1)} %copy-done.27, ...), custom_call_target="tpu_custom_call" | custom-call | bytes 4718592 | tf_op jit(solution)/shard_map/pallas_call | solution.py:51
  (200 shorter events, 61.0 us)
Async XLA Ops:
  0.6 23.5 %collective-permute-start.17 = (bf16[256,3072]{1,0:T(8,128)(2,1)}, bf16[256,3072]{1,0:T(8,128)(2,1)S(1)}, u32[]{:S(2)}, u32[]{:S(2)}) collective-permute-start(bf16[256,3072]{1,0:T(8,128)(2,1)} %refs_1_.1), channel_id=1, source_target_pairs={{0,16},{2,18},{16,0},{18,2},{4,20},{6,22},{20,4},{22,6},{8,24},{10... | collective-permute-start | bytes 4718600 | tf_op jit(solution)/shard_map/ppermute | solution.py:362
  24.1 36.4 %collective-permute-start.18 = (bf16[256,3072]{1,0:T(8,128)(2,1)S(1)}, bf16[256,3072]{1,0:T(8,128)(2,1)S(1)}, u32[]{:S(2)}, u32[]{:S(2)}) collective-permute-start(bf16[256,3072]{1,0:T(8,128)(2,1)S(1)} %collective-permute-done.17.refs_5_.refs_2_), channel_id=1, source_target_pairs={{0,1},{2,3},{4,5},{6,7},{8,9},{10,11},{12,13},{14,15},{16,17},{18,... | collective-permute-start | bytes 4718600 | tf_op jit(solution)/shard_map/ppermute | solution.py:363
  30.0 14.3 %collective-permute-start.5 = (bf16[2,2,384,128]{3,2,1,0:T(8,128)(2,1)}, bf16[2,2,384,128]{3,2,1,0:T(8,128)(2,1)}, u32[]{:S(2)}, u32[]{:S(2)}) collective-permute-start(bf16[2,2,384,128]{3,2,1,0:T(8,128)(2,1)} %get-tuple-element.43), channel_id=1, source_target_pairs={{0,2},{1,3},{2,0},{3,1},{4,6},{5,7},{6,4},{7,5},{8,10},{9,11},{10,... | collective-permute-start | bytes 1179656 | tf_op jit(solution)/shard_map/ppermute | solution.py:18
  30.1 18.0 %collective-permute-start.3 = (bf16[2,2,384,128]{3,2,1,0:T(8,128)(2,1)}, bf16[2,2,384,128]{3,2,1,0:T(8,128)(2,1)}, u32[]{:S(2)}, u32[]{:S(2)}) collective-permute-start(bf16[2,2,384,128]{3,2,1,0:T(8,128)(2,1)} %get-tuple-element.42.refs_8_.refs_4_), channel_id=1, source_target_pairs={{0,4},{4,8},{8,12},{1,5},{5,9},{9,13},{2,6},{6,10},{10,14},{3,7},{... | collective-permute-start | bytes 1179656 | tf_op jit(solution)/shard_map/ppermute | solution.py:24
  34.7 14.6 %collective-permute-start.8 = (bf16[2,2,384,128]{3,2,1,0:T(8,128)(2,1)}, bf16[2,2,384,128]{3,2,1,0:T(8,128)(2,1)}, u32[]{:S(2)}, u32[]{:S(2)}) collective-permute-start(bf16[2,2,384,128]{3,2,1,0:T(8,128)(2,1)} %get-tuple-element.42.refs_8_.refs_4_), channel_id=1, source_target_pairs={{0,1},{1,0},{2,3},{3,2},{4,5},{5,4},{6,7},{7,6},{8,9},{9,8},{10,11... | collective-permute-start | bytes 1179656 | tf_op jit(solution)/shard_map/ppermute | solution.py:18
  38.1 14.2 %collective-permute-start.10 = (bf16[2,2,384,128]{3,2,1,0:T(8,128)(2,1)}, bf16[2,2,384,128]{3,2,1,0:T(8,128)(2,1)}, u32[]{:S(2)}, u32[]{:S(2)}) collective-permute-start(bf16[2,2,384,128]{3,2,1,0:T(8,128)(2,1)} %get-tuple-element.42.refs_8_.refs_4_), channel_id=1, source_target_pairs={{4,0},{8,4},{12,8},{5,1},{9,5},{13,9},{6,2},{10,6},{14,10},{7,3},{... | collective-permute-start | bytes 1179656 | tf_op jit(solution)/shard_map/ppermute | solution.py:24
  44.3 12.2 %collective-permute-start.6 = (bf16[2,2,384,128]{3,2,1,0:T(8,128)(2,1)}, bf16[2,2,384,128]{3,2,1,0:T(8,128)(2,1)S(1)}, u32[]{:S(2)}, u32[]{:S(2)}) collective-permute-start(bf16[2,2,384,128]{3,2,1,0:T(8,128)(2,1)} %collective-permute-done.5.refs_10_.refs_6_), channel_id=1, source_target_pairs={{0,4},{4,8},{8,12},{1,5},{5,9},{9,13},{2,6},{6,10},{10,14},{3,7},{... | collective-permute-start | bytes 1179656 | tf_op jit(solution)/shard_map/ppermute | solution.py:24
  48.0 12.5 %collective-permute-start.12 = (bf16[2,2,384,128]{3,2,1,0:T(8,128)(2,1)}, bf16[2,2,384,128]{3,2,1,0:T(8,128)(2,1)S(1)}, u32[]{:S(2)}, u32[]{:S(2)}) collective-permute-start(bf16[2,2,384,128]{3,2,1,0:T(8,128)(2,1)} %collective-permute-done.5.refs_10_.refs_6_), channel_id=1, source_target_pairs={{4,0},{8,4},{12,8},{5,1},{9,5},{13,9},{6,2},{10,6},{14,10},{7,3},{... | collective-permute-start | bytes 1179656 | tf_op jit(solution)/shard_map/ppermute | solution.py:24
  52.2 61.2 %collective-permute-start.30 = (bf16[384,1536]{1,0:T(8,128)(2,1)S(1)}, bf16[384,1536]{1,0:T(8,128)(2,1)}, u32[]{:S(2)}, u32[]{:S(2)}) collective-permute-start(bf16[384,1536]{1,0:T(8,128)(2,1)S(1)} %get-tuple-element.75), channel_id=1, source_target_pairs={{0,1},{1,0},{2,3},{3,2},{4,5},{5,4},{6,7},{7,6},{8,9},{9,8},{10,11... | collective-permute-start | bytes 3538952 | tf_op jit(solution)/shard_map/ppermute | solution.py:18
  52.8 14.9 %collective-permute-start.9 = (bf16[2,2,384,128]{3,2,1,0:T(8,128)(2,1)}, bf16[2,2,384,128]{3,2,1,0:T(8,128)(2,1)S(1)}, u32[]{:S(2)}, u32[]{:S(2)}) collective-permute-start(bf16[2,2,384,128]{3,2,1,0:T(8,128)(2,1)} %collective-permute-done.5.refs_10_.refs_6_), channel_id=1, source_target_pairs={{0,1},{1,0},{2,3},{3,2},{4,5},{5,4},{6,7},{7,6},{8,9},{9,8},{10,11... | collective-permute-start | bytes 1179656 | tf_op jit(solution)/shard_map/ppermute | solution.py:18
  56.5 12.9 %collective-permute-start.11 = (bf16[2,2,384,128]{3,2,1,0:T(8,128)(2,1)}, bf16[2,2,384,128]{3,2,1,0:T(8,128)(2,1)S(1)}, u32[]{:S(2)}, u32[]{:S(2)}) collective-permute-start(bf16[2,2,384,128]{3,2,1,0:T(8,128)(2,1)} %collective-permute-done.10.refs_12_.refs_4_), channel_id=1, source_target_pairs={{0,1},{1,0},{2,3},{3,2},{4,5},{5,4},{6,7},{7,6},{8,9},{9,8},{10,11... | collective-permute-start | bytes 1179656 | tf_op jit(solution)/shard_map/ppermute | solution.py:18
  67.8 14.7 %collective-permute-start.20 = (bf16[2,384,128]{2,1,0:T(8,128)(2,1)}, bf16[2,384,128]{2,1,0:T(8,128)(2,1)S(1)}, u32[]{:S(2)}, u32[]{:S(2)}) collective-permute-start(bf16[2,384,128]{2,1,0:T(8,128)(2,1)} %get-tuple-element.47), channel_id=1, source_target_pairs={{0,2},{1,3},{2,0},{3,1},{4,6},{5,7},{6,4},{7,5},{8,10},{9,11},{10,... | collective-permute-start | bytes 589832 | tf_op jit(solution)/shard_map/ppermute | solution.py:18
  83.0 30.5 %collective-permute-start.14 = (bf16[2,384,128]{2,1,0:T(8,128)(2,1)}, bf16[2,384,128]{2,1,0:T(8,128)(2,1)S(1)}, u32[]{:S(2)}, u32[]{:S(2)}) collective-permute-start(bf16[2,384,128]{2,1,0:T(8,128)(2,1)} %get-tuple-element.44.refs_0_), channel_id=1, source_target_pairs={{0,1},{1,0},{2,3},{3,2},{4,5},{5,4},{6,7},{7,6},{8,9},{9,8},{10,11... | collective-permute-start | bytes 589832 | tf_op jit(solution)/shard_map/ppermute | solution.py:18
  89.2 24.3 %collective-permute-start.16 = (bf16[2,384,128]{2,1,0:T(8,128)(2,1)S(1)}, bf16[2,384,128]{2,1,0:T(8,128)(2,1)S(1)}, u32[]{:S(2)}, u32[]{:S(2)}) collective-permute-start(bf16[2,384,128]{2,1,0:T(8,128)(2,1)S(1)} %collective-permute-done.15.refs_2_.refs_1_), channel_id=1, source_target_pairs={{0,1},{1,0},{2,3},{3,2},{4,5},{5,4},{6,7},{7,6},{8,9},{9,8},{10,11... | collective-permute-start | bytes 589832 | tf_op jit(solution)/shard_map/ppermute | solution.py:18
  103.6 53.5 %collective-permute-start.25 = (bf16[2,1536,128]{2,1,0:T(8,128)(2,1)}, bf16[2,1536,128]{2,1,0:T(8,128)(2,1)S(1)}, u32[]{:S(2)}, u32[]{:S(2)}) collective-permute-start(bf16[2,1536,128]{2,1,0:T(8,128)(2,1)} %get-tuple-element.56), channel_id=1, source_target_pairs={{0,4},{4,8},{8,12},{1,5},{5,9},{9,13},{2,6},{6,10},{10,14},{3,7},{... | collective-permute-start | bytes 2359304 | tf_op jit(solution)/shard_map/ppermute | solution.py:24
  112.2 44.9 %collective-permute-start.26 = (bf16[2,1536,128]{2,1,0:T(8,128)(2,1)S(1)}, bf16[2,1536,128]{2,1,0:T(8,128)(2,1)S(1)}, u32[]{:S(2)}, u32[]{:S(2)}) collective-permute-start(bf16[2,1536,128]{2,1,0:T(8,128)(2,1)S(1)} %copy-done.49), channel_id=1, source_target_pairs={{4,0},{8,4},{12,8},{5,1},{9,5},{13,9},{6,2},{10,6},{14,10},{7,3},{... | collective-permute-start | bytes 2359304 | tf_op jit(solution)/shard_map/ppermute | solution.py:24
  119.2 11.4 %collective-permute-start.31 = (bf16[256,768]{1,0:T(8,128)(2,1)}, bf16[256,768]{1,0:T(8,128)(2,1)S(1)}, u32[]{:S(2)}, u32[]{:S(2)}) collective-permute-start(bf16[256,768]{1,0:T(8,128)(2,1)} %get-tuple-element.64), channel_id=1, source_target_pairs={{0,16},{16,0},{1,17},{17,1},{2,18},{18,2},{3,19},{19,3},{4,20},{20... | collective-permute-start | bytes 1179656 | tf_op jit(solution)/shard_map/ppermute | solution.py:18
  144.4 18.3 %collective-permute-start.37 = (bf16[32,1536]{1,0:T(8,128)(2,1)}, bf16[32,1536]{1,0:T(8,128)(2,1)S(1)}, u32[]{:S(2)}, u32[]{:S(2)}) collective-permute-start(bf16[32,1536]{1,0:T(8,128)(2,1)} %get-tuple-element.74), channel_id=1, source_target_pairs={{0,12},{4,8},{8,4},{12,0},{1,13},{5,9},{9,5},{13,1},{2,14},{6,10},... | collective-permute-start | bytes 294920 | tf_op jit(solution)/shard_map/ppermute | solution.py:18
  147.5 15.2 %collective-permute-start.36 = (bf16[32,1536]{1,0:T(8,128)(2,1)}, bf16[32,1536]{1,0:T(8,128)(2,1)S(1)}, u32[]{:S(2)}, u32[]{:S(2)}) collective-permute-start(bf16[32,1536]{1,0:T(8,128)(2,1)} %get-tuple-element.73), channel_id=1, source_target_pairs={{0,8},{4,12},{8,0},{12,4},{1,9},{5,13},{9,1},{13,5},{2,10},{6,14},... | collective-permute-start | bytes 294920 | tf_op jit(solution)/shard_map/ppermute | solution.py:18
  148.2 14.5 %collective-permute-start.35 = (bf16[32,1536]{1,0:T(8,128)(2,1)}, bf16[32,1536]{1,0:T(8,128)(2,1)S(1)}, u32[]{:S(2)}, u32[]{:S(2)}) collective-permute-start(bf16[32,1536]{1,0:T(8,128)(2,1)} %get-tuple-element.72), channel_id=1, source_target_pairs={{0,4},{4,0},{8,12},{12,8},{1,5},{5,1},{9,13},{13,9},{2,6},{6,2},{1... | collective-permute-start | bytes 294920 | tf_op jit(solution)/shard_map/ppermute | solution.py:18
  161.2 20.1 %collective-permute-start.28 = (bf16[2,2,384,128]{3,2,1,0:T(8,128)(2,1)}, bf16[2,2,384,128]{3,2,1,0:T(8,128)(2,1)S(1)}, u32[]{:S(2)}, u32[]{:S(2)}) collective-permute-start(bf16[2,2,384,128]{3,2,1,0:T(8,128)(2,1)} %get-tuple-element.59), channel_id=1, source_target_pairs={{0,2},{1,3},{2,0},{3,1},{4,6},{5,7},{6,4},{7,5},{8,10},{9,11},{10,... | collective-permute-start | bytes 1179656 | tf_op jit(solution)/shard_map/ppermute | solution.py:18
  181.3 16.7 %collective-permute-start.27 = (bf16[2,2,384,128]{3,2,1,0:T(8,128)(2,1)}, bf16[2,2,384,128]{3,2,1,0:T(8,128)(2,1)S(1)}, u32[]{:S(2)}, u32[]{:S(2)}) collective-permute-start(bf16[2,2,384,128]{3,2,1,0:T(8,128)(2,1)} %get-tuple-element.58.refs_4_), channel_id=1, source_target_pairs={{0,1},{1,0},{2,3},{3,2},{4,5},{5,4},{6,7},{7,6},{8,9},{9,8},{10,11... | collective-permute-start | bytes 1179656 | tf_op jit(solution)/shard_map/ppermute | solution.py:18
  181.3 16.7 %collective-permute-start.29 = (bf16[2,2,384,128]{3,2,1,0:T(8,128)(2,1)S(1)}, bf16[2,2,384,128]{3,2,1,0:T(8,128)(2,1)S(1)}, u32[]{:S(2)}, u32[]{:S(2)}) collective-permute-start(bf16[2,2,384,128]{3,2,1,0:T(8,128)(2,1)S(1)} %collective-permute-done.28.refs_6_), channel_id=1, source_target_pairs={{0,1},{1,0},{2,3},{3,2},{4,5},{5,4},{6,7},{7,6},{8,9},{9,8},{10,11... | collective-permute-start | bytes 1179656 | tf_op jit(solution)/shard_map/ppermute | solution.py:18
  184.8 13.1 %collective-permute-start.22 = (bf16[2,384,128]{2,1,0:T(8,128)(2,1)S(1)}, bf16[2,384,128]{2,1,0:T(8,128)(2,1)S(1)}, u32[]{:S(2)}, u32[]{:S(2)}) collective-permute-start(bf16[2,384,128]{2,1,0:T(8,128)(2,1)S(1)} %copy-done.24), channel_id=1, source_target_pairs={{0,1},{1,0},{2,3},{3,2},{4,5},{5,4},{6,7},{7,6},{8,9},{9,8},{10,11... | collective-permute-start | bytes 589832 | tf_op jit(solution)/shard_map/ppermute | solution.py:18
  (80 other events, 573.8 us)
